TPU v7x, 256 devices: a whole 4x4x8 slice. The times are simulated.
256 devices in a mesh: group: 8 (over y, core), ctx: 32 (over z, x).
Axes of the slice: x: 4, y: 4, z: 8, core: 2. Of those that a mesh axis runs over, the one named last changes fastest.
Arguments:
- query_raw: bfloat16 [8, 512, 4096], P('group', 'ctx'), may hold values from -6 to 6
- suffix_keyval: bfloat16 [8, 512, 1024], P('group', 'ctx'), may hold values from -12 to 12
- query_gain: float32 [128], replicated, may hold values from 0.5 to 1.5
- key_norm_gain: float32 [128], replicated, may hold values from 1.5 to 4
- positions: int32 [8, 512], P('group', 'ctx'), may hold values from 8192 to 25087, as said below
- prefix_length: int32 [8], P('group'), may hold values from 8192 to 24576
- page_owner: int32 [8, 1536, 1], P('group', 'ctx'), may hold values from 0 to 7; in each aligned block of 48 rows (0 to 47, 48 to 95, ..., all dimensions but the last counted through in order) at most 12 rows name the same one
- page_slot: int32 [8, 1536], P('group', 'ctx'), may hold values from 0 to 95
- cache_pool: bfloat16 [8, 3072, 16, 1024], P('group', 'ctx'), may hold values from -22 to 22
Outputs:
- attention_out: bfloat16 [8, 512, 4096], P('group', 'ctx')
Inputs may be any that keep to these rules, and one draw needn't show every extreme that they name: positions[g, i] = prefix_length[g] + i. `page_owner`: among the 48 pages of one device (aligned blocks of pages), at most 12 name the same owner group.
All inputs are finite; a program needn't handle non-finite values.
Results may differ from a plain program's by a relative error of at most 0.02.
Values may be sent and summed in bfloat16 or wider, within the bound.
A program may use at most 128 MiB of HBM per device.

v0:
```python
import jax
import jax.numpy as jnp
from jax import lax
from jax.sharding import Mesh
from jax.sharding import PartitionSpec as P

CTX = ("ctx_0", "ctx_1")


epsilon = 1e-06
floor_score = -1e30


def gather_axes(array, axes, dim):
    for axis in reversed(axes):
        array = lax.all_gather(array, axis, axis=dim, tiled=True)
    return array


def from_everyone(array, axis):
    copies = jnp.broadcast_to(array, (lax.axis_size(axis), *array.shape))
    return lax.all_to_all(copies, axis, split_axis=0, concat_axis=0, tiled=True)


def of_everyone(array, axis):
    return from_everyone(array, axis).max(axis=0)


def summed_rows(array, axes, dim):
    if not axes:
        return array
    nearer = lax.psum_scatter(array, axes[0], scatter_dimension=dim, tiled=True)
    return summed_rows(nearer, axes[1:], dim)


def apply_rotation(raw_rows, gain, token_places):
    head_width = raw_rows.shape[-1]
    half_width = head_width // 2
    scaled = (
        raw_rows * lax.rsqrt(jnp.mean(raw_rows * raw_rows, axis=-1, keepdims=True) + epsilon) * gain
    )
    frequency = 1000000.0 ** (-(2.0 / head_width) * jnp.arange(half_width, dtype=jnp.float32))
    angles = token_places.astype(jnp.float32)[:, None] * frequency[None, :]
    cosine = jnp.cos(angles)[:, None, :]
    sine_part = jnp.sin(angles)[:, None, :]
    lower_half = scaled[..., :half_width]
    upper_half = scaled[..., half_width:]
    return jnp.concatenate(
        [
            lower_half * cosine - upper_half * sine_part,
            upper_half * cosine + lower_half * sine_part,
        ],
        axis=-1,
    )


def attend(running, query_rows, rows_block, visible, score_scale):
    row_best, row_total, row_accum = running
    key_heads = query_rows.shape[1]
    head_width = query_rows.shape[3]
    key_value_split = key_heads * head_width
    key_rows = rows_block[:, :key_value_split].reshape(-1, key_heads, head_width)
    value_rows = rows_block[:, key_value_split:].reshape(-1, key_heads, head_width)
    scores = (
        jnp.einsum("qhjd,khd->qhjk", query_rows, key_rows, preferred_element_type=jnp.float32)
        * score_scale
    )
    shown_mask = visible[:, None, None, :]
    scores = jnp.where(shown_mask, scores, floor_score)
    raised = jnp.maximum(row_best, jnp.max(scores, axis=-1))
    weights = jnp.where(shown_mask, jnp.exp(scores - raised[..., None]), 0.0)
    row_total = jnp.sum(weights, axis=-1)
    row_accum = jnp.einsum(
        "qhjk,khd->qhjd",
        weights.astype(jnp.bfloat16),
        value_rows,
        preferred_element_type=jnp.float32,
    )
    return (raised, row_total, row_accum)


def visibility(owner_shard, query_index, local_rows, shard_len, prefix_limit, block_rows):
    position = jnp.arange(block_rows, dtype=jnp.int32)
    prefix_ok = owner_shard * local_rows + position < prefix_limit
    suffix_key = owner_shard * shard_len + position - local_rows
    return jnp.where(
        (position < local_rows)[None, :],
        prefix_ok[None, :],
        suffix_key[None, :] <= query_index[:, None],
    )


def shards(
    query_raw,
    suffix_keyval,
    query_gain,
    key_norm_gain,
    positions,
    prefix_length,
    page_owner,
    page_slot,
    cache_pool,
):
    shard_len = query_raw.shape[1]
    head_width = query_gain.shape[0]
    key_value_split = suffix_keyval.shape[2] // 2
    key_heads = key_value_split // head_width
    query_heads = query_raw.shape[2] // head_width
    query_group_ratio = query_heads // key_heads
    score_scale = head_width ** (-0.5)
    token_places = positions[0]
    query_rot = apply_rotation(
        query_raw[0].astype(jnp.float32).reshape(shard_len, query_heads, head_width),
        query_gain,
        token_places,
    )
    query_rot = query_rot.astype(jnp.bfloat16).reshape(shard_len, query_heads * head_width)
    key_rotated = apply_rotation(
        suffix_keyval[0, :, :key_value_split]
        .astype(jnp.float32)
        .reshape(shard_len, key_heads, head_width),
        key_norm_gain,
        token_places,
    )
    key_rotated = key_rotated.astype(jnp.bfloat16).reshape(shard_len, key_value_split)
    newest_rows = jnp.concatenate([key_rotated, suffix_keyval[0, :, key_value_split:]], axis=1)
    group_count = lax.axis_size("group")
    pages_dev = page_slot.shape[1]
    capacity = max(2, 2 * pages_dev // group_count)
    owner_ids = page_owner[0, :, 0]
    slot_ids = page_slot[0]
    onehot = (owner_ids[:, None] == jnp.arange(group_count, dtype=jnp.int32)[None, :]).astype(
        jnp.int32
    )
    before = jnp.cumsum(onehot, axis=0) - onehot
    rank_ids = jnp.sum(before * onehot, axis=1)
    requests = (
        jnp.zeros((group_count * capacity,), jnp.int32)
        .at[owner_ids * capacity + rank_ids]
        .set(slot_ids)
    )
    requests = requests.reshape(group_count, capacity)
    local_pool = cache_pool[0]
    served = local_pool[lax.all_to_all(requests, "group", split_axis=0, concat_axis=0, tiled=True)]
    arrived = lax.all_to_all(served, "group", split_axis=0, concat_axis=0, tiled=True)
    pulled = arrived[owner_ids, rank_ids]
    local_rows = pages_dev * local_pool.shape[1]
    prefix_rows = pulled.reshape(local_rows, pulled.shape[2])
    local_block = jnp.concatenate([prefix_rows, newest_rows], axis=0)
    block_rows = local_rows + shard_len
    ctx_index = lax.axis_index(CTX)
    prefix_limit = prefix_length[0]
    every_query = gather_axes(query_rot, CTX, 0)
    total_queries = every_query.shape[0]
    size_block = min(total_queries, 128)
    block_count = total_queries // size_block
    query_blocks = every_query.reshape(
        block_count, size_block, key_heads, query_group_ratio, head_width
    )
    index_blocks = jnp.arange(total_queries, dtype=jnp.int32).reshape(block_count, size_block)

    def local_part(inputs):
        chosen, indices = inputs
        visible = visibility(ctx_index, indices, local_rows, shard_len, prefix_limit, block_rows)
        initial = (
            jnp.full((size_block, key_heads, query_group_ratio), floor_score, jnp.float32),
            jnp.zeros((size_block, key_heads, query_group_ratio), jnp.float32),
            jnp.zeros((size_block, key_heads, query_group_ratio, head_width), jnp.float32),
        )
        return attend(initial, chosen, local_block, visible, score_scale)

    row_best, row_total, row_accum = lax.map(local_part, (query_blocks, index_blocks))
    row_best = row_best.reshape(total_queries, query_heads)
    row_total = row_total.reshape(total_queries, query_heads)
    row_accum = row_accum.reshape(total_queries, query_heads, head_width)
    peak = of_everyone(row_best.astype(jnp.bfloat16), CTX).astype(row_best.dtype)
    factor = jnp.exp(row_best - peak)
    weighted = (row_accum * factor[..., None]).reshape(total_queries, query_heads * head_width)
    summed, totals = (
        summed_rows(weighted.astype(jnp.bfloat16), CTX, 0).astype(jnp.float32),
        summed_rows((row_total * factor).astype(jnp.bfloat16), CTX, 0).astype(jnp.float32),
    )
    result = (summed.reshape(shard_len, query_heads, head_width) / totals[..., None]).reshape(
        shard_len, query_heads * head_width
    )
    return result.astype(jnp.bfloat16).reshape(1, shard_len, query_heads * head_width)


def solution(mesh):
    finer = Mesh(mesh.devices.reshape(mesh.shape["group"], 8, 4), ("group", "ctx_0", "ctx_1"))
    in_specs = (
        P("group", CTX, None),
        P("group", CTX, None),
        P(),
        P(),
        P("group", CTX),
        P("group"),
        P("group", CTX, None),
        P("group", CTX),
        P("group", CTX, None, None),
    )
    out_specs = P("group", CTX, None)
    return jax.shard_map(
        shards, mesh=finer, in_specs=in_specs, out_specs=out_specs, check_vma=False
    )
```

profile of v0, /device:TPU:1, one launch (start us, length us, event | category | flops | bytes accessed | tf_op | source)
XLA Modules:
  0.0 392.4 jit_solution(17780011511473687665)
XLA Ops:
  9.8 12.8 %all_gather.6 = bf16[64,4096]{1,0:T(8,128)(2,1)} all-gather(bf16[16,4096]{1,0:T(8,128)(2,1)S(1)} %bitcast.151), channel_id=1, replica_groups=mesh['group'=8,'ctx_0'=8,'ctx_1'=4] {'ctx_1'}, dimensions={0}, use_global_device_ids=true | all-gather | bytes 655360 | tf_op jit(solution)/shard_map/all_gather | solution.py:16
  25.8 11.4 %all_to_all.22 = s32[8,1,12]{2,1,0:T(1,128)S(1)} all-to-all(s32[8,1,12]{2,1,0:T(1,128)S(1)} %bitcast.158), channel_id=1, replica_groups=mesh['group'=8,'ctx_0'=8,'ctx_1'=4] {'group'}, dimensions={0} | all-to-all | bytes 768 | tf_op jit(solution)/shard_map/all_to_all | solution.py:144
  44.7 37.0 %all-to-all-done.1 = bf16[8,12,16,1024]{3,2,1,0:T(8,128)(2,1)S(1)} async-done(((bf16[8,12,16,1024]{3,2,1,0:T(8,128)(2,1)}), bf16[8,12,16,1024]{3,2,1,0:T(8,128)(2,1)S(1)}, u32[]{:S(2)}, u32[]{:S(2)}) %all-to-all-start.1) | async-done | bytes 3145760 | tf_op jit(solution)/shard_map/all_to_all | solution.py:145
  91.9 112.9 %while.16 = (s32[]{:T(128)}, f32[4,128,4,8]{1,0,3,2:T(4,128)S(1)}, f32[4,128,4,8]{1,0,3,2:T(4,128)S(1)}, f32[4,128,4,8,128]{4,3,2,1,0:T(8,128)}, s32[]{:T(128)},...) while((s32[]{:T(128)}, f32[4,128,4,8]{1,0,3,2:T(4,128)S(1)}, ...), condition=%wide.region_8.9_spmd, body=%wide.region_5.8_spmd.sunk | while | flops 1686114048 | bytes 56576860 | solution.py:172
  96.3 5.8 %bitcast_reduce_fusion.2 = (f32[128,4,8]{0,2,1:T(8,128)S(1)}, f32[4,128,8,784]{1,3,2,0:T(8,128)}) fusion(pred[128,784]{0,1:T(8,128)(4,1)S(1)} %compare_select_fusion.6, bf16[784,4,128,1]{2,1,0,3:T(4,128)(2,1)S(1)} %bitcast.139, bf16[1,128,4,8,128]{4,3,2,1,0:T(8,128)(2,1)S(1)} %constant_dynamic-slice_fusion.3), kind=kOutput, calls=%fused_computation.4.clone.1 | convolution fusion | flops 831713280 | bytes 14813184 | tf_op jit(solution)/shard_map/while/body/eval_jaxpr/qhjd,khd->qhjk/dot_general | solution.py:65
  102.2 7.8 %fusion.45 = f32[128,4,8]{0,2,1:T(8,128)S(1)} fusion(f32[4,128,8,784]{1,3,2,0:T(8,128)} %get-tuple-element.269, f32[128,4,8]{0,2,1:T(8,128)S(1)} %broadcast_maximum_fusion.2, pred[128,784]{0,1:T(8,128)(4,1)S(1)} %compare_select_fusion.6), kind=kLoop, calls=%fused_computation.9.clone.1 | loop fusion | flops 16052224 | bytes 12978176 | tf_op jit(solution)/shard_map/while/body/eval_jaxpr/reduce_sum | solution.py:72
  110.3 7.3 %fusion.46 = f32[1,128,4,8,128]{4,1,3,2,0:T(8,128)S(1)} fusion(f32[4,128,8,784]{1,3,2,0:T(8,128)} %get-tuple-element.269, f32[128,4,8]{0,2,1:T(8,128)S(1)} %broadcast_maximum_fusion.2, pred[128,784]{0,1:T(8,128)(4,1)S(1)} %compare_select_fusion.6, bf16[784,4,128,1]{2,1,0,3:T(4,128)(2,1)S(1)} %bitcast.142), kind=kOutput, calls=%fused_computation.14.clone.1 | convolution fusion | flops 838139904 | bytes 15861760 | tf_op jit(solution)/shard_map/while/body/eval_jaxpr/qhjk,khd->qhjd/dot_general | solution.py:73
  124.5 5.8 %bitcast_reduce_fusion.2 = (f32[128,4,8]{0,2,1:T(8,128)S(1)}, f32[4,128,8,784]{1,3,2,0:T(8,128)}) fusion(pred[128,784]{0,1:T(8,128)(4,1)S(1)} %compare_select_fusion.6, bf16[784,4,128,1]{2,1,0,3:T(4,128)(2,1)S(1)} %bitcast.139, bf16[1,128,4,8,128]{4,3,2,1,0:T(8,128)(2,1)S(1)} %constant_dynamic-slice_fusion.3), kind=kOutput, calls=%fused_computation.4.clone.1 | convolution fusion | flops 831713280 | bytes 14813184 | tf_op jit(solution)/shard_map/while/body/eval_jaxpr/qhjd,khd->qhjk/dot_general | solution.py:65
  130.5 7.8 %fusion.45 = f32[128,4,8]{0,2,1:T(8,128)S(1)} fusion(f32[4,128,8,784]{1,3,2,0:T(8,128)} %get-tuple-element.269, f32[128,4,8]{0,2,1:T(8,128)S(1)} %broadcast_maximum_fusion.2, pred[128,784]{0,1:T(8,128)(4,1)S(1)} %compare_select_fusion.6), kind=kLoop, calls=%fused_computation.9.clone.1 | loop fusion | flops 16052224 | bytes 12978176 | tf_op jit(solution)/shard_map/while/body/eval_jaxpr/reduce_sum | solution.py:72
  138.5 7.3 %fusion.46 = f32[1,128,4,8,128]{4,1,3,2,0:T(8,128)S(1)} fusion(f32[4,128,8,784]{1,3,2,0:T(8,128)} %get-tuple-element.269, f32[128,4,8]{0,2,1:T(8,128)S(1)} %broadcast_maximum_fusion.2, pred[128,784]{0,1:T(8,128)(4,1)S(1)} %compare_select_fusion.6, bf16[784,4,128,1]{2,1,0,3:T(4,128)(2,1)S(1)} %bitcast.142), kind=kOutput, calls=%fused_computation.14.clone.1 | convolution fusion | flops 838139904 | bytes 15861760 | tf_op jit(solution)/shard_map/while/body/eval_jaxpr/qhjk,khd->qhjd/dot_general | solution.py:73
  152.8 5.8 %bitcast_reduce_fusion.2 = (f32[128,4,8]{0,2,1:T(8,128)S(1)}, f32[4,128,8,784]{1,3,2,0:T(8,128)}) fusion(pred[128,784]{0,1:T(8,128)(4,1)S(1)} %compare_select_fusion.6, bf16[784,4,128,1]{2,1,0,3:T(4,128)(2,1)S(1)} %bitcast.139, bf16[1,128,4,8,128]{4,3,2,1,0:T(8,128)(2,1)S(1)} %constant_dynamic-slice_fusion.3), kind=kOutput, calls=%fused_computation.4.clone.1 | convolution fusion | flops 831713280 | bytes 14813184 | tf_op jit(solution)/shard_map/while/body/eval_jaxpr/qhjd,khd->qhjk/dot_general | solution.py:65
  158.7 7.8 %fusion.45 = f32[128,4,8]{0,2,1:T(8,128)S(1)} fusion(f32[4,128,8,784]{1,3,2,0:T(8,128)} %get-tuple-element.269, f32[128,4,8]{0,2,1:T(8,128)S(1)} %broadcast_maximum_fusion.2, pred[128,784]{0,1:T(8,128)(4,1)S(1)} %compare_select_fusion.6), kind=kLoop, calls=%fused_computation.9.clone.1 | loop fusion | flops 16052224 | bytes 12978176 | tf_op jit(solution)/shard_map/while/body/eval_jaxpr/reduce_sum | solution.py:72
  166.7 7.3 %fusion.46 = f32[1,128,4,8,128]{4,1,3,2,0:T(8,128)S(1)} fusion(f32[4,128,8,784]{1,3,2,0:T(8,128)} %get-tuple-element.269, f32[128,4,8]{0,2,1:T(8,128)S(1)} %broadcast_maximum_fusion.2, pred[128,784]{0,1:T(8,128)(4,1)S(1)} %compare_select_fusion.6, bf16[784,4,128,1]{2,1,0,3:T(4,128)(2,1)S(1)} %bitcast.142), kind=kOutput, calls=%fused_computation.14.clone.1 | convolution fusion | flops 838139904 | bytes 15861760 | tf_op jit(solution)/shard_map/while/body/eval_jaxpr/qhjk,khd->qhjd/dot_general | solution.py:73
  181.0 5.8 %bitcast_reduce_fusion.2 = (f32[128,4,8]{0,2,1:T(8,128)S(1)}, f32[4,128,8,784]{1,3,2,0:T(8,128)}) fusion(pred[128,784]{0,1:T(8,128)(4,1)S(1)} %compare_select_fusion.6, bf16[784,4,128,1]{2,1,0,3:T(4,128)(2,1)S(1)} %bitcast.139, bf16[1,128,4,8,128]{4,3,2,1,0:T(8,128)(2,1)S(1)} %constant_dynamic-slice_fusion.3), kind=kOutput, calls=%fused_computation.4.clone.1 | convolution fusion | flops 831713280 | bytes 14813184 | tf_op jit(solution)/shard_map/while/body/eval_jaxpr/qhjd,khd->qhjk/dot_general | solution.py:65
  186.9 7.8 %fusion.45 = f32[128,4,8]{0,2,1:T(8,128)S(1)} fusion(f32[4,128,8,784]{1,3,2,0:T(8,128)} %get-tuple-element.269, f32[128,4,8]{0,2,1:T(8,128)S(1)} %broadcast_maximum_fusion.2, pred[128,784]{0,1:T(8,128)(4,1)S(1)} %compare_select_fusion.6), kind=kLoop, calls=%fused_computation.9.clone.1 | loop fusion | flops 16052224 | bytes 12978176 | tf_op jit(solution)/shard_map/while/body/eval_jaxpr/reduce_sum | solution.py:72
  195.0 7.3 %fusion.46 = f32[1,128,4,8,128]{4,1,3,2,0:T(8,128)S(1)} fusion(f32[4,128,8,784]{1,3,2,0:T(8,128)} %get-tuple-element.269, f32[128,4,8]{0,2,1:T(8,128)S(1)} %broadcast_maximum_fusion.2, pred[128,784]{0,1:T(8,128)(4,1)S(1)} %compare_select_fusion.6, bf16[784,4,128,1]{2,1,0,3:T(4,128)(2,1)S(1)} %bitcast.142), kind=kOutput, calls=%fused_computation.14.clone.1 | convolution fusion | flops 838139904 | bytes 15861760 | tf_op jit(solution)/shard_map/while/body/eval_jaxpr/qhjk,khd->qhjd/dot_general | solution.py:73
  206.0 11.1 %all-to-all-start.2 = ((bf16[32,512,32]{1,2,0:T(8,128)(2,1)}), bf16[32,512,32]{1,2,0:T(8,128)(2,1)S(1)}, u32[]{:S(2)}, u32[]{:S(2)}) async-start(bf16[32,512,32]{1,2,0:T(8,128)(2,1)} %broadcast_in_dim.120), calls=%async_computation.2 | async-start | bytes 2097152 | tf_op jit(solution)/shard_map/all_to_all | solution.py:22
  217.2 9.4 %reshape.334 = f32[512,4096]{1,0:T(8,128)} reshape(f32[4,128,4,8,128]{4,3,2,1,0:T(8,128)} %get-tuple-element.127) | data formatting | bytes 16777216 | tf_op jit(solution)/shard_map/reshape | solution.py:175
  226.6 16.6 %all-to-all-done.2 = bf16[32,512,32]{1,2,0:T(8,128)(2,1)S(1)} async-done(((bf16[32,512,32]{1,2,0:T(8,128)(2,1)}), bf16[32,512,32]{1,2,0:T(8,128)(2,1)S(1)}, u32[]{:S(2)}, u32[]{:S(2)}) %all-to-all-start.2) | async-done | bytes 1048608 | tf_op jit(solution)/shard_map/all_to_all | solution.py:22
  250.2 12.6 %fusion.18 = bf16[512,4096]{1,0:T(8,128)(2,1)} fusion(f32[512,4096]{1,0:T(8,128)} %reshape.334, f32[64,8,32,128]{3,2,1,0:T(8,128)} %bitcast.140), kind=kLoop, calls=%fused_computation.31 | loop fusion | flops 4194304 | bytes 20971520 | tf_op jit(solution)/shard_map/convert_element_type | solution.py:180
  263.0 10.3 %reduce-scatter.13.cloned.1.call-done = bf16[64,32]{1,0:T(8,128)(2,1)} async-done(((bf16[512,32]{1,0:T(8,128)(2,1)}), bf16[64,32]{1,0:T(8,128)(2,1)}) %reduce-scatter.13.cloned.1.call-update) | async-done | bytes 4112
  273.3 62.0 %reduce-scatter.9.cloned.1.call-done = bf16[64,4096]{1,0:T(8,128)(2,1)} async-done(((bf16[512,4096]{1,0:T(8,128)(2,1)}), bf16[64,4096]{1,0:T(8,128)(2,1)}) %reduce-scatter.9.cloned.1.call-update) | async-done | bytes 524304 | tf_op jit(solution)/shard_map/reduce_scatter | solution.py:32
  335.3 21.8 %reduce-scatter.15.cloned.1.call-done = bf16[16,32]{1,0:T(8,128)(2,1)} async-done(((bf16[64,32]{1,0:T(8,128)(2,1)}), bf16[16,32]{1,0:T(8,128)(2,1)}) %reduce-scatter.15.cloned.1.call-update) | async-done | bytes 1040 | tf_op jit(solution)/shard_map/reduce_scatter | solution.py:32
  357.1 26.3 %reduce-scatter.11.cloned.1.call-done = bf16[16,4096]{1,0:T(8,128)(2,1)} async-done(((bf16[64,4096]{1,0:T(8,128)(2,1)}), bf16[16,4096]{1,0:T(8,128)(2,1)}) %reduce-scatter.11.cloned.1.call-update) | async-done | bytes 131088 | tf_op jit(solution)/shard_map/reduce_scatter | solution.py:32
  (113 shorter events, 63.9 us)
Async XLA Ops:
  6.5 30.8 %copy-start = (bf16[1,96,16,1024]{3,2,1,0:T(8,128)(2,1)S(1)}, bf16[1,96,16,1024]{3,2,1,0:T(8,128)(2,1)}, u32[]{:S(2)}) copy-start(bf16[1,96,16,1024]{3,2,1,0:T(8,128)(2,1)} %param.19) | copy-start | bytes 9437188
  6.5 79.9 %all-gather.2.cloned.1.call-start = ((), (), s32[]{:S(2)}) async-start(), calls=%async_computation.7 | async-start | bytes 4718592 | tf_op jit(solution)/shard_map/all_gather | solution.py:16
  7.6 36.6 %copy-start.2 = (bf16[1,16,1024]{2,1,0:T(8,128)(2,1)S(1)}, bf16[1,16,1024]{2,1,0:T(8,128)(2,1)}, u32[]{:S(2)}) copy-start(bf16[1,16,1024]{2,1,0:T(8,128)(2,1)} %param.12) | copy-start | bytes 98308
  7.6 36.7 %copy-start.3 = (f32[128]{0:T(128)S(1)}, f32[128]{0:T(128)}, u32[]{:S(2)}) copy-start(f32[128]{0:T(128)} %param.14) | copy-start | bytes 1540
  40.0 41.7 %all-to-all-start.1 = ((bf16[8,12,16,1024]{3,2,1,0:T(8,128)(2,1)}), bf16[8,12,16,1024]{3,2,1,0:T(8,128)(2,1)S(1)}, u32[]{:S(2)}, u32[]{:S(2)}) async-start(bf16[8,12,16,1024]{3,2,1,0:T(8,128)(2,1)} %bitcast.143), calls=%async_computation.1 | async-start | bytes 6291456 | tf_op jit(solution)/shard_map/all_to_all | solution.py:145
  206.0 37.2 %all-to-all-start.2 = ((bf16[32,512,32]{1,2,0:T(8,128)(2,1)}), bf16[32,512,32]{1,2,0:T(8,128)(2,1)S(1)}, u32[]{:S(2)}, u32[]{:S(2)}) async-start(bf16[32,512,32]{1,2,0:T(8,128)(2,1)} %broadcast_in_dim.120), calls=%async_computation.2 | async-start | bytes 2097152 | tf_op jit(solution)/shard_map/all_to_all | solution.py:22
  217.2 56.1 %reduce-scatter.13.cloned.1.call-start = ((), (), s32[]{:S(2)}) async-start(), calls=%async_computation.10 | async-start | bytes 147456
  244.2 91.1 %reduce-scatter.9.cloned.1.call-start = ((), (), s32[]{:S(2)}) async-start(), calls=%async_computation.8 | async-start | bytes 4718592 | tf_op jit(solution)/shard_map/reduce_scatter | solution.py:32
  250.2 135.7 %copy-start.1 = (bf16[1,96,16,1024]{3,2,1,0:T(8,128)(2,1)S(1)}, bf16[1,96,16,1024]{3,2,1,0:T(8,128)(2,1)}, u32[]{:S(2)}) copy-start(bf16[1,96,16,1024]{3,2,1,0:T(8,128)(2,1)} %param.19) | copy-start | bytes 9437188
  262.9 94.2 %reduce-scatter.15.cloned.1.call-start = ((), (), s32[]{:S(2)}) async-start(), calls=%async_computation.11 | async-start | bytes 20480 | tf_op jit(solution)/shard_map/reduce_scatter | solution.py:32
  273.3 110.1 %reduce-scatter.11.cloned.1.call-start = ((), (), s32[]{:S(2)}) async-start(), calls=%async_computation.9 | async-start | bytes 655360 | tf_op jit(solution)/shard_map/reduce_scatter | solution.py:32
Sparse Core Ops, SparseCore 0:
  22.7 59.5 all-gather.1
  244.3 28.8 reduce-scatter.12
  275.8 59.4 reduce-scatter.8
  337.6 19.4 reduce-scatter.14
  359.5 23.8 reduce-scatter.10
where the time goes:
time: 395 us; the launch traced here: 392 us
  waiting for transfers between devices  174 us (44%)
  other arithmetic  59.7 us (15%)
  local copies, waits for them, and re-layouts  52.7 us (13%)
  matrix products  52.4 us (13%)
  blocking collectives  24.2 us (6%)
  starting transfers between devices  15.7 us (4%)
  between operations  13.3 us (3%)
    reduce_scatter x3, waiting for transfers between devices, summed_rows(): nearer = lax.psum_scatter(array, axes[0], scatter_dimension=dim, tiled=True)  110 us
    all_to_all x1, waiting for transfers between devices, shards(): lax.all_to_all(served, 'group', split_axis=0, concat_axis=0, tiled=True)  37 us
    reduce_sum x4, other arithmetic, attend(): row_total = jnp.sum(weights, axis=-1)  31.1 us
    dot_general x4, matrix products, attend(): jnp.einsum('qhjk,khd->qhjd', weights.astype(jnp.bfloat16), value_rows, pr...  29.2 us
    dot_general x4, matrix products, attend(): jnp.einsum('qhjd,khd->qhjk', query_rows, key_rows, preferred_element_type...  23.3 us
    all_to_all x1, waiting for transfers between devices, from_everyone(): return lax.all_to_all(copies, axis, split_axis=0, concat_axis=0, tiled=True)  16.6 us
    all_gather x1, blocking collectives, gather_axes(): array = lax.all_gather(array, axis, axis=dim, tiled=True)  12.8 us
    convert_element_type x1, other arithmetic, shards(): weighted.astype(jnp.bfloat16)  12.6 us
  transfers between devices with their start and end apart: 7, of which 6 were waited for; matrix products, arithmetic and copies ran while one was open for 10% of the time, Pallas kernels for 0%

commit v1 on v0

v1 whole, which is shorter than its diff:
```python
import jax
import jax.numpy as jnp
from jax import lax
from jax.experimental import pallas as pl
from jax.experimental.pallas import tpu as pltpu
from jax.sharding import Mesh
from jax.sharding import PartitionSpec as P

MESH = pl.DeviceIdType.MESH
EPS = 1e-06
FLOOR = -1e30
GROUPS = 8
ROWS = 8
COLS = 4
CAP = 12
PAGES = 48
PAGE = 16
HEAD = 128
TOKENS = 16
RATIO = 8
KEYS = PAGES * PAGE
BLOCK = COLS * RATIO * TOKENS
HALF = BLOCK // 2
SUMROWS = 16
F32 = jnp.float32
BF16 = jnp.bfloat16


def rot(a, n):
    return lax.rem(a, jnp.int32(n))


def kernel(
    tab, cs, qraw, skv, qgain, kgain, plen, pool, out,
    send0, send1, send2, send3, recv0, recv1, recv2, recv3,
    kc, vc, vt, ks, vs, qsend, qbuf, oacc, mref, osend, stsend, orecv, strecv, fsend, frecv,
    reqv, reqs, idxv, idxs,
    psend, precv, lsem, rsend, rrecv, isend, irecv, ssem, xsend, xrecv,
    upsend, uprecv, dnsend, dnrecv, osem, orsem, tsem, trsem, fsem, frsem,
):
    g = lax.axis_index("group")
    z = lax.axis_index("ctx_0")
    x = lax.axis_index("ctx_1")
    sends = (send0, send1, send2, send3)
    recvs = (recv0, recv1, recv2, recv3)
    limit = plen[0]

    barrier = pltpu.get_barrier_semaphore()

    @pl.loop(1, GROUPS * COLS)
    def _(n):
        to = (rot(g + n // COLS, GROUPS), z, rot(x + rot(n, COLS), COLS))
        pl.semaphore_signal(barrier, inc=1, device_id=to, device_id_type=MESH)

    @pl.loop(1, ROWS)
    def _(n):
        pl.semaphore_signal(
            barrier, inc=1, device_id=(g, rot(z + n, ROWS), x), device_id_type=MESH
        )

    cosf = cs[0]
    sinf = cs[1]
    scale = HEAD ** (-0.5) * 1.4426950408889634

    def turned(raw, gain):
        raw = raw.astype(F32)
        mean = jnp.mean(raw * raw, axis=-1, keepdims=True)
        flat = raw * lax.rsqrt(mean + EPS) * gain
        return flat * cosf + pltpu.roll(flat, HEAD // 2, 1) * sinf

    for i in range(COLS * RATIO):
        part = turned(qraw[:, i * HEAD : (i + 1) * HEAD], qgain[...])
        qsend[i // RATIO, i % RATIO] = (part * scale).astype(BF16)
    for i in range(COLS):
        part = turned(skv[:, i * HEAD : (i + 1) * HEAD], kgain[...])
        qsend[i, RATIO] = part.astype(BF16)
        qsend[i, RATIO + 1] = skv[:, (COLS + i) * HEAD : (COLS + i + 1) * HEAD]

    pl.semaphore_wait(barrier, GROUPS * COLS - 1 + ROWS - 1)

    def req_copy(d):
        to = rot(g + d, GROUPS)
        return pltpu.make_async_remote_copy(
            src_ref=tab.at[to], dst_ref=reqv.at[g], send_sem=rsend.at[d], recv_sem=rrecv.at[d],
            device_id=(to, z, x), device_id_type=MESH,
        )

    def idx_copy(k):
        return pltpu.make_async_remote_copy(
            src_ref=tab.at[GROUPS], dst_ref=idxv.at[k], send_sem=isend.at[k], recv_sem=irecv.at[k],
            device_id=(g, z, rot(x + k, COLS)), device_id_type=MESH,
        )

    mine = z * COLS + x

    def q_copy(k):
        to = rot(x + k, COLS)
        return pltpu.make_async_remote_copy(
            src_ref=qsend.at[to], dst_ref=qbuf.at[mine], send_sem=xsend.at[k], recv_sem=xrecv.at[k],
            device_id=(g, z, to), device_id_type=MESH,
        )

    for d in range(1, GROUPS):
        req_copy(d).start()
    for k in range(1, COLS):
        idx_copy(k).start()
    for k in range(1, COLS):
        q_copy(k).start()

    def ring_copy(s, k, up):
        col = rot(x + COLS - k, COLS)
        away = rot(z + ROWS - s, ROWS) if up else rot(z + s, ROWS)
        place = away * COLS + col
        if s == 0 and k == 0:
            src = qsend.at[x, pl.ds(0, RATIO + 1)]
        else:
            src = qbuf.at[place, pl.ds(0, RATIO + 1)]
        to = rot(z + 1, ROWS) if up else rot(z + ROWS - 1, ROWS)
        return pltpu.make_async_remote_copy(
            src_ref=src, dst_ref=qbuf.at[place, pl.ds(0, RATIO + 1)],
            send_sem=(upsend if up else dnsend).at[s, k],
            recv_sem=(uprecv if up else dnrecv).at[s, k],
            device_id=(g, to, x), device_id_type=MESH,
        )

    ring_copy(0, 0, True).start()
    ring_copy(0, 0, False).start()
    qbuf[mine] = qsend[x]

    own_req = pltpu.make_async_copy(tab.at[g], reqs.at[g], ssem.at[0])
    own_idx = pltpu.make_async_copy(tab.at[GROUPS], idxs.at[0], ssem.at[GROUPS])
    own_req.start()
    own_idx.start()

    def req_local(d):
        frm = rot(g + GROUPS - d, GROUPS)
        return pltpu.make_async_copy(reqv.at[frm], reqs.at[frm], ssem.at[d])

    for d in range(1, GROUPS):
        req_copy(d).wait_recv()
        req_local(d).start()
    own_req.wait()
    for d in range(1, GROUPS):
        req_local(d).wait()

    def page_copy(k, d):
        to = rot(g + d, GROUPS)
        return pltpu.make_async_remote_copy(
            src_ref=sends[k].at[pl.ds(to * CAP, CAP)], dst_ref=recvs[k].at[pl.ds(g * CAP, CAP)],
            send_sem=psend.at[k, d], recv_sem=precv.at[k, d],
            device_id=(to, z, rot(x + k, COLS)), device_id_type=MESH,
        )

    own_pages = pltpu.make_async_copy(
        send0.at[pl.ds(g * CAP, CAP)], recv0.at[pl.ds(g * CAP, CAP)], lsem.at[0]
    )

    def gather(k):
        head = rot(x + k, COLS)
        key_at = pl.multiple_of(head * HEAD, HEAD)
        value_at = pl.multiple_of((COLS + head) * HEAD, HEAD)

        @pl.loop(0, GROUPS)
        def _(d):
            to = rot(g + d, GROUPS)
            for r in range(CAP):
                slot = reqs[to, 0, r]
                sends[k][to * CAP + r, :, 0:HEAD] = pool[slot, :, pl.ds(key_at, HEAD)]
                sends[k][to * CAP + r, :, HEAD : 2 * HEAD] = pool[slot, :, pl.ds(value_at, HEAD)]
            if k:
                page_copy(k, d).start()
            else:

                @pl.when(d > 0)
                def _():
                    page_copy(0, d).start()

    for k in range(COLS):
        gather(k)
    own_pages.start()

    for k in range(1, COLS):
        q_copy(k).wait_recv()
        ring_copy(0, k, True).start()
        ring_copy(0, k, False).start()
    for s in range(1, 5):
        for k in range(COLS):
            ring_copy(s - 1, k, True).wait_recv()
            if s < 4:
                ring_copy(s, k, True).start()
            if s < 4:
                ring_copy(s - 1, k, False).wait_recv()
            if s < 3:
                ring_copy(s, k, False).start()

    for k in range(1, COLS):
        idx_copy(k).wait_recv()
        pltpu.make_async_copy(idxv.at[k], idxs.at[k], ssem.at[GROUPS + k]).start()
    own_idx.wait()
    for k in range(1, COLS):
        pltpu.make_async_copy(idxv.at[k], idxs.at[k], ssem.at[GROUPS + k]).wait()

    def queries(zb, c):
        part = qbuf[pl.ds(zb * COLS + 2 * c, 2), 0:RATIO]
        return part.reshape(HALF, HEAD)

    def logits(keys, zb, c):
        return lax.dot_general(
            keys, queries(zb, c), (((1,), (1,)), ((), ())), preferred_element_type=F32
        )

    for b in range(COLS):
        ks[b * TOKENS : (b + 1) * TOKENS] = qbuf[z * COLS + b, RATIO]
        vs[b * TOKENS : (b + 1) * TOKENS] = qbuf[z * COLS + b, RATIO + 1].astype(F32)
    ks[COLS * TOKENS :] = jnp.zeros((HEAD - COLS * TOKENS, HEAD), BF16)
    vs[COLS * TOKENS :] = jnp.zeros((HEAD - COLS * TOKENS, HEAD), F32)
    suffix_t = jnp.concatenate(
        [vs[...].T.astype(BF16), jnp.ones((SUMROWS, HEAD), BF16)], axis=0
    )
    suffix_k = ks[...]

    @pl.loop(0, ROWS)
    def _(zb):
        for c in range(2):
            key_row = lax.broadcasted_iota(jnp.int32, (HEAD, HALF), 0)
            column = lax.broadcasted_iota(jnp.int32, (HEAD, HALF), 1)
            asker = zb * (COLS * TOKENS) + (column // HEAD + 2 * c) * TOKENS + (column & (TOKENS - 1))
            seen = (key_row < COLS * TOKENS) & (z * (COLS * TOKENS) + key_row <= asker)
            s = jnp.where(seen, logits(suffix_k, zb, c), FLOOR)
            peak = jnp.max(s, axis=0, keepdims=True)
            p = jnp.exp2(s - peak).astype(BF16)
            at = slice(c * HALF, (c + 1) * HALF)
            mref[zb, 0:1, at] = peak
            oacc[zb, :, at] = jnp.dot(suffix_t, p, preferred_element_type=F32)

    shared_key = qbuf[0, RATIO][0:1, :].astype(F32)

    def compact(k):
        col = rot(x + COLS - k, COLS)
        base = (z * COLS + col) * KEYS

        @pl.loop(0, PAGES)
        def _(j):
            page = recvs[k][idxs[k, 0, j]].astype(F32)
            token = base + j * PAGE + lax.broadcasted_iota(jnp.int32, (PAGE, HEAD), 0)
            seen = token < limit
            rows = pl.ds(pl.multiple_of(j * PAGE, PAGE), PAGE)
            kc[rows, :] = jnp.where(seen, page[:, 0:HEAD], shared_key).astype(BF16)
            vc[rows, :] = jnp.where(seen, page[:, HEAD:], 0.0)

        lane = base + lax.broadcasted_iota(jnp.int32, (SUMROWS, KEYS), 1)
        for b in range(KEYS // HEAD):
            vt[0:HEAD, b * HEAD : (b + 1) * HEAD] = vc[b * HEAD : (b + 1) * HEAD, :].T.astype(BF16)
        vt[HEAD:, :] = jnp.where(lane < limit, 1.0, 0.0).astype(BF16)

    def attend(zb):
        for c in range(2):
            at = slice(c * HALF, (c + 1) * HALF)
            s = logits(kc[...], zb, c)
            before = mref[zb, 0:1, at]
            peak = jnp.maximum(before, jnp.max(s, axis=0, keepdims=True))
            p = jnp.exp2(s - peak).astype(BF16)
            fresh = jnp.dot(vt[...], p, preferred_element_type=F32)
            oacc[zb, :, at] = oacc[zb, :, at] * jnp.exp2(before - peak) + fresh
            mref[zb, 0:1, at] = peak

    def o_copy(off):
        to = rot(z + off, ROWS)
        return pltpu.make_async_remote_copy(
            src_ref=osend.at[to], dst_ref=orecv.at[off], send_sem=osem.at[off], recv_sem=orsem.at[off],
            device_id=(g, to, x), device_id_type=MESH,
        )

    def t_copy(off):
        to = rot(z + off, ROWS)
        return pltpu.make_async_remote_copy(
            src_ref=stsend.at[to], dst_ref=strecv.at[off], send_sem=tsem.at[off], recv_sem=trsem.at[off],
            device_id=(g, to, x), device_id_type=MESH,
        )

    for k in range(COLS):
        if k == 0:
            own_pages.wait()
        for d in range(0 if k else 1, GROUPS):
            page_copy(k, d).wait_recv()
        compact(k)
        if k < COLS - 1:

            @pl.loop(0, ROWS)
            def _(zb):
                attend(zb)

        else:

            @pl.loop(0, ROWS)
            def _(n):
                off = 4 + (1 - 2 * rot(n, 2)) * ((n + 1) // 2)
                zb = rot(z + off, ROWS)
                attend(zb)
                osend[zb] = oacc[zb, 0:HEAD, :].astype(BF16)
                stsend[zb, 0:1, :] = mref[zb, 0:1, :]
                stsend[zb, 1:2, :] = oacc[zb, HEAD : HEAD + 1, :]

                @pl.when(n < ROWS - 1)
                def _():
                    t_copy(off).start()
                    o_copy(off).start()

    for off in range(1, ROWS):
        t_copy(off).wait_recv()
    peaks = [stsend[z, 0:1, :]] + [strecv[off, 0:1, :] for off in range(1, ROWS)]
    sums = [stsend[z, 1:2, :]] + [strecv[off, 1:2, :] for off in range(1, ROWS)]
    top = peaks[0]
    for off in range(1, ROWS):
        top = jnp.maximum(top, peaks[off])
    parts = [jnp.exp2(peak - top) for peak in peaks]
    total = parts[0] * sums[0]
    for off in range(1, ROWS):
        total = total + parts[off] * sums[off]
    joined = osend[z].astype(F32) * parts[0]
    for off in (1, 7, 2, 6, 3, 5, 4):
        o_copy(off).wait_recv()
        joined = joined + orecv[off].astype(F32) * parts[off]
    joined = joined / total
    for b in range(COLS):
        block = joined[:, b * HEAD : (b + 1) * HEAD].T.astype(BF16)
        fsend[b] = block.reshape(RATIO, TOKENS, HEAD)

    def f_copy(k):
        to = rot(x + k, COLS)
        return pltpu.make_async_remote_copy(
            src_ref=fsend.at[to], dst_ref=frecv.at[x], send_sem=fsem.at[k], recv_sem=frsem.at[k],
            device_id=(g, z, to), device_id_type=MESH,
        )

    for k in range(1, COLS):
        f_copy(k).start()
    frecv[x] = fsend[x]
    for k in range(1, COLS):
        f_copy(k).wait_recv()
    for h in range(COLS):
        for i in range(RATIO):
            at = (h * RATIO + i) * HEAD
            out[:, at : at + HEAD] = frecv[h, i]

    for d in range(1, GROUPS):
        req_copy(d).wait_send()
    for k in range(1, COLS):
        idx_copy(k).wait_send()
        q_copy(k).wait_send()
        f_copy(k).wait_send()
    for s in range(4):
        for k in range(COLS):
            ring_copy(s, k, True).wait_send()
            if s < 3:
                ring_copy(s, k, False).wait_send()
    for k in range(COLS):
        for d in range(0 if k else 1, GROUPS):
            page_copy(k, d).wait_send()
    for off in range(1, ROWS):
        t_copy(off).wait_send()
        o_copy(off).wait_send()


def shards(
    query_raw, suffix_keyval, query_gain, key_norm_gain, positions, prefix_length,
    page_owner, page_slot, cache_pool,
):
    half = HEAD // 2
    frequency = 1000000.0 ** (-(2.0 / HEAD) * jnp.arange(half, dtype=F32))
    angles = positions[0].astype(F32)[:, None] * frequency[None, :]
    cosine, sine = jnp.cos(angles), jnp.sin(angles)
    cs = jnp.stack(
        [jnp.concatenate([cosine, cosine], axis=1), jnp.concatenate([-sine, sine], axis=1)]
    )
    owner = page_owner[0, :, 0]
    slot = page_slot[0]
    order = jnp.arange(PAGES, dtype=jnp.int32)
    same = (owner[:, None] == owner[None, :]) & (order[None, :] < order[:, None])
    place = owner * CAP + jnp.sum(same.astype(jnp.int32), axis=1)
    lanes = jnp.arange(HEAD, dtype=jnp.int32)
    wanted = jnp.where(
        lanes < CAP, jnp.arange(GROUPS, dtype=jnp.int32)[:, None] * CAP + lanes[None, :], -1
    )
    hit = wanted[:, :, None] == place[None, None, :]
    requests = jnp.sum(jnp.where(hit, slot[None, None, :], 0), axis=2)
    places = jnp.pad(place, (0, HEAD - PAGES))[None]
    tab = jnp.concatenate([requests, places], axis=0)
    tab = jnp.broadcast_to(tab[:, None, :], (GROUPS + 1, 8, HEAD))
    vmem = pl.BlockSpec(memory_space=pltpu.VMEM)
    page_half = (GROUPS * CAP, PAGE, 2 * HEAD)
    dma = pltpu.SemaphoreType.DMA
    result = pl.pallas_call(
        kernel,
        out_shape=jax.ShapeDtypeStruct((TOKENS, COLS * RATIO * HEAD), BF16),
        in_specs=[vmem] * 6 + [pl.BlockSpec(memory_space=pltpu.SMEM), vmem],
        out_specs=vmem,
        scratch_shapes=[pltpu.VMEM(page_half, BF16)] * 8
        + [
            pltpu.VMEM((KEYS, HEAD), BF16),
            pltpu.VMEM((KEYS, HEAD), F32),
            pltpu.VMEM((HEAD + SUMROWS, KEYS), BF16),
            pltpu.VMEM((HEAD, HEAD), BF16),
            pltpu.VMEM((HEAD, HEAD), F32),
            pltpu.VMEM((COLS, RATIO + 2, TOKENS, HEAD), BF16),
            pltpu.VMEM((ROWS * COLS, RATIO + 2, TOKENS, HEAD), BF16),
            pltpu.VMEM((ROWS, HEAD + SUMROWS, BLOCK), F32),
            pltpu.VMEM((ROWS, 8, BLOCK), F32),
            pltpu.VMEM((ROWS, HEAD, BLOCK), BF16),
            pltpu.VMEM((ROWS, 8, BLOCK), F32),
            pltpu.VMEM((ROWS, HEAD, BLOCK), BF16),
            pltpu.VMEM((ROWS, 8, BLOCK), F32),
            pltpu.VMEM((COLS, RATIO, TOKENS, HEAD), BF16),
            pltpu.VMEM((COLS, RATIO, TOKENS, HEAD), BF16),
            pltpu.VMEM((GROUPS, 8, HEAD), jnp.int32),
            pltpu.SMEM((GROUPS, 8, HEAD), jnp.int32),
            pltpu.VMEM((COLS, 8, HEAD), jnp.int32),
            pltpu.SMEM((COLS, 8, HEAD), jnp.int32),
            dma((COLS, GROUPS)), dma((COLS, GROUPS)), dma((1,)),
            dma((GROUPS,)), dma((GROUPS,)), dma((COLS,)), dma((COLS,)), dma((GROUPS + COLS,)),
            dma((COLS,)), dma((COLS,)),
            dma((4, COLS)), dma((4, COLS)), dma((3, COLS)), dma((3, COLS)),
            dma((ROWS,)), dma((ROWS,)), dma((ROWS,)), dma((ROWS,)),
            dma((COLS,)), dma((COLS,)),
        ],
        compiler_params=pltpu.CompilerParams(
            collective_id=0, has_side_effects=True, vmem_limit_bytes=60 * 1024 * 1024
        ),
        name="spanned",
    )(
        tab, cs, query_raw[0], suffix_keyval[0], query_gain[None], key_norm_gain[None],
        prefix_length, cache_pool[0],
    )
    return result[None]


def solution(mesh):
    finer = Mesh(mesh.devices.reshape(GROUPS, ROWS, COLS), ("group", "ctx_0", "ctx_1"))
    ctx = ("ctx_0", "ctx_1")
    in_specs = (
        P("group", ctx, None),
        P("group", ctx, None),
        P(),
        P(),
        P("group", ctx),
        P("group"),
        P("group", ctx, None),
        P("group", ctx),
        P("group", ctx, None, None),
    )
    return jax.shard_map(
        shards, mesh=finer, in_specs=in_specs, out_specs=P("group", ctx, None), check_vma=False
    )
```

time: 395 us -> 126 us (0.32)
  waiting for transfers between devices: 174 us -> 0 us
  Pallas kernels: 0 us -> 119 us
  other arithmetic: 59.7 us -> 3.88 us
  matrix products: 52.4 us -> 0 us
  local copies, waits for them, and re-layouts: 52.7 us -> 2.19 us
  blocking collectives: 24.2 us -> 0 us
  starting transfers between devices: 15.7 us -> 0 us
  between operations: 13.3 us -> 0.69 us
    pallas_call x0 -> x1, Pallas kernels: none -> 119 us  [shards(): pl.pallas_call(kernel, out_shape=jax.ShapeDtypeStruct((TOKENS, COLS * RAT...]
    reduce_scatter x3 -> x0, waiting for transfers between devices: 110 us -> none  [summed_rows(): nearer = lax.psum_scatter(array, axes[0], scatter_dimension=dim, tiled=True)]
    all_to_all x2 -> x0, waiting for transfers between devices: 53.6 us -> none  [the longest x1 37 us: shards(): lax.all_to_all(served, 'group', split_axis=0, concat_axis=0, tiled=True)]
    dot_general x8 -> x0, matrix products: 52.4 us -> none  [the longest x4 29.2 us: attend(): jnp.einsum('qhjk,khd->qhjd', weights.astype(jnp.bfloat16), value_rows, pr...]
    reduce_sum x7 -> x2, other arithmetic: 32.2 us -> 1.65 us  [the longest x1 0.91 us: shards(): place = owner * CAP + jnp.sum(same.astype(jnp.int32), axis=1)]
    all_to_all x2 -> x0, starting transfers between devices: 15.4 us -> none  [the longest x1 11.1 us: from_everyone(): return lax.all_to_all(copies, axis, split_axis=0, concat_axis=0, tiled=True)]
    convert_element_type x5 -> x1, other arithmetic: 14.1 us -> 0.66 us  [shards(): angles = positions[0].astype(F32)[:, None] * frequency[None, :]]
    all_gather x1 -> x0, blocking collectives: 12.8 us -> none  [gather_axes(): array = lax.all_gather(array, axis, axis=dim, tiled=True)]
  transfers between devices with their start and end apart: 7 -> 0, of which waited for: 6 -> 0; matrix products, arithmetic and copies ran while one was open for 10% -> 0% of each run, Pallas kernels for 0% -> 0%
where the time goes in v1:
time: 126 us
  Pallas kernels  119 us (94%)
  other arithmetic  3.88 us (3%)
  local copies, waits for them, and re-layouts  2.19 us (2%)
    pallas_call x1, Pallas kernels, shards(): pl.pallas_call(kernel, out_shape=jax.ShapeDtypeStruct((TOKENS, COLS * RAT...  119 us

profile of v1, /device:TPU:1, one launch (start us, length us, event | category | flops | bytes accessed | tf_op | source)
XLA Modules:
  0.0 125.6 jit_solution(14117478149223351181)
XLA Ops:
  0.7 0.7 convert_bitcast_fusion
  1.3 0.9 convert_reduce_fusion
  2.2 0.7 multiply_add_fusion
  2.9 0.1 add_select_fusion
  3.0 0.7 select_reduce_fusion
  3.8 0.1 multiply_cosine_fusion
  3.9 0.1 maximum_bitcast_fusion
  4.0 0.6 pad_maximum_fusion.cs
  4.6 0.6 broadcast_in_dim.54.tab
  5.2 118.9 %spanned.1 = bf16[16,4096]{1,0:T(8,128)(2,1)} custom-call(s32[9,8,128]{2,1,0:T(8,128)} %broadcast_in_dim.54.tab, f32[2,16,128]{2,1,0:T(8,128)} %pad_maximum_fusion.cs, bf16[16,4096]{1,0:T(8,128)(2,1)} %bitcast.19, bf16[16,1024]{1,0:T(8,128)(2,1)} %bitcast.20, f32[1,128]{1,0:T(1,128)} %bitcast.22, f32[1,128]{1,0:T(1,128)} %bitcast.23, s32[1]{0:T(128)S(6)} %copy.11.plen, ...), custom_call_target="tpu_custom_call" | custom-call | tf_op jit(solution)/shard_map/spanned/pallas_call | solution.py:393
  124.1 1.6 %copy.12 = bf16[1,16,4096]{2,1,0:T(8,128)(2,1)} copy(bf16[1,16,4096]{2,1,0:T(8,128)(2,1)} %bitcast.18) | data formatting | bytes 262144
  (5 shorter events, 0.0 us)

commit v2 on v1

v2 whole, which is shorter than its diff:
```python
import jax
import jax.numpy as jnp
from jax import lax
from jax.experimental import pallas as pl
from jax.experimental.pallas import tpu as pltpu
from jax.sharding import Mesh
from jax.sharding import PartitionSpec as P

MESH = pl.DeviceIdType.MESH
EPS = 1e-06
FLOOR = -65536.0
GROUPS = 8
ROWS = 8
COLS = 4
CAP = 12
PAGES = 48
POOL = 96
PAGE = 16
HEAD = 128
TOKENS = 16
RATIO = 8
KEYS = PAGES * PAGE
BLOCK = COLS * RATIO * TOKENS
HALF = BLOCK // 2
SUMROWS = 16
WIDE = KEYS + HEAD
LAST = (4, 5, 3, 6, 2, 7, 1, 0)
F32 = jnp.float32
BF16 = jnp.bfloat16


def rot(a, n):
    return lax.rem(a, jnp.int32(n))


def kernel(
    tab, cs, qraw, skv, qgain, kgain, plen, pool_any, out,
    pool, send0, send1, send2, send3, recv0, recv1, recv2, recv3,
    near0, near1, near2, near3, cut1, cut2, cut3,
    kc, vt, sa, sb, pa, pb, qsend, qbuf, oacc, mref, osend, upin, dnin, fsend, frecv,
    reqv, reqs, idxs,
    psend, precv, lsem, rsend, rrecv, ssem, xsend, xrecv,
    upsend, uprecv, dnsend, dnrecv, nsend, nrecv, uosend, uorecv, dosend, dorecv, fsem, frsem,
):
    g = lax.axis_index("group")
    z = lax.axis_index("ctx_0")
    x = lax.axis_index("ctx_1")
    sends = (send0, send1, send2, send3)
    recvs = (recv0, recv1, recv2, recv3)
    nears = (near0, near1, near2, near3)
    cuts = (near0, cut1, cut2, cut3)
    limit = plen[0]
    up_z, down_z = rot(z + 1, ROWS), rot(z + ROWS - 1, ROWS)

    load_pool = pltpu.make_async_copy(pool_any, pool, lsem.at[COLS])
    load_pool.start()
    barrier = pltpu.get_barrier_semaphore()
    partners = [(rot(g + n, GROUPS), z, x) for n in range(1, GROUPS)]
    partners += [(g, z, rot(x + n, COLS)) for n in range(1, COLS)]
    partners += [(g, up_z, x), (g, down_z, x)]
    for to in partners:
        pl.semaphore_signal(barrier, inc=1, device_id=to, device_id_type=MESH)

    cosf = cs[0]
    sinf = cs[1]
    scale = HEAD ** (-0.5) * 1.4426950408889634

    def turned(raw, gain):
        raw = raw.astype(F32)
        mean = jnp.mean(raw * raw, axis=-1, keepdims=True)
        flat = raw * lax.rsqrt(mean + EPS) * gain
        return flat * cosf + pltpu.roll(flat, HEAD // 2, 1) * sinf

    for i in range(COLS * RATIO):
        part = turned(qraw[:, i * HEAD : (i + 1) * HEAD], qgain[...])
        qsend[i // RATIO, i % RATIO] = (part * scale).astype(BF16)
    for i in range(COLS):
        part = turned(skv[:, i * HEAD : (i + 1) * HEAD], kgain[...])
        qsend[i, RATIO] = part.astype(BF16)
        qsend[i, RATIO + 1] = skv[:, (COLS + i) * HEAD : (COLS + i + 1) * HEAD]

    pl.semaphore_wait(barrier, len(partners))

    def req_copy(d):
        to = rot(g + d, GROUPS)
        return pltpu.make_async_remote_copy(
            src_ref=tab.at[to], dst_ref=reqv.at[g], send_sem=rsend.at[d], recv_sem=rrecv.at[d],
            device_id=(to, z, x), device_id_type=MESH,
        )

    mine = z * COLS + x

    def q_copy(k):
        to = rot(x + k, COLS)
        return pltpu.make_async_remote_copy(
            src_ref=qsend.at[to], dst_ref=qbuf.at[mine], send_sem=xsend.at[k], recv_sem=xrecv.at[k],
            device_id=(g, z, to), device_id_type=MESH,
        )

    for d in range(1, GROUPS):
        req_copy(d).start()
    for k in range(1, COLS):
        q_copy(k).start()

    def ring_copy(s, k, up):
        col = rot(x + COLS - k, COLS)
        away = rot(z + ROWS - s, ROWS) if up else rot(z + s, ROWS)
        place = away * COLS + col
        if s == 0 and k == 0:
            src = qsend.at[x, pl.ds(0, RATIO + 1)]
        else:
            src = qbuf.at[place, pl.ds(0, RATIO + 1)]
        return pltpu.make_async_remote_copy(
            src_ref=src, dst_ref=qbuf.at[place, pl.ds(0, RATIO + 1)],
            send_sem=(upsend if up else dnsend).at[s, k],
            recv_sem=(uprecv if up else dnrecv).at[s, k],
            device_id=(g, up_z if up else down_z, x), device_id_type=MESH,
        )

    ring_copy(0, 0, True).start()
    ring_copy(0, 0, False).start()
    qbuf[mine] = qsend[x]

    own_req = pltpu.make_async_copy(tab.at[g], reqs.at[g], ssem.at[0])
    own_idx = pltpu.make_async_copy(tab.at[GROUPS], idxs, ssem.at[GROUPS])
    own_req.start()
    own_idx.start()

    def req_local(d):
        frm = rot(g + GROUPS - d, GROUPS)
        return pltpu.make_async_copy(reqv.at[frm], reqs.at[frm], ssem.at[d])

    for d in range(1, GROUPS):
        req_copy(d).wait_recv()
        req_local(d).start()
    own_req.wait()
    own_idx.wait()
    for d in range(1, GROUPS):
        req_local(d).wait()
    load_pool.wait()

    def page_copy(k, d):
        to = rot(g + d, GROUPS)
        return pltpu.make_async_remote_copy(
            src_ref=sends[k].at[pl.ds(to * CAP, CAP)], dst_ref=recvs[k].at[pl.ds(g * CAP, CAP)],
            send_sem=psend.at[k, d], recv_sem=precv.at[k, d],
            device_id=(to, z, x), device_id_type=MESH,
        )

    def own_pages(k):
        own = pl.ds(g * CAP, CAP)
        return pltpu.make_async_copy(sends[k].at[own], recvs[k].at[own], lsem.at[k])

    def gather(k):
        head = rot(x + k, COLS)
        key_at = pl.multiple_of(head * HEAD, HEAD)
        value_at = pl.multiple_of((COLS + head) * HEAD, HEAD)

        @pl.loop(0, GROUPS)
        def _(d):
            to = rot(g + d, GROUPS)
            for r in range(CAP):
                slot = reqs[to, 0, r]
                sends[k][to * CAP + r, :, 0:HEAD] = pool[slot, :, pl.ds(key_at, HEAD)]
                sends[k][to * CAP + r, :, HEAD : 2 * HEAD] = pool[slot, :, pl.ds(value_at, HEAD)]

            @pl.when(d > 0)
            def _():
                page_copy(k, d).start()

        own_pages(k).start()

    for k in (1, 2, 3, 0):
        gather(k)

    def near_copy(k):
        return pltpu.make_async_remote_copy(
            src_ref=cuts[k], dst_ref=nears[k], send_sem=nsend.at[k], recv_sem=nrecv.at[k],
            device_id=(g, z, rot(x + k, COLS)), device_id_type=MESH,
        )

    def compact(k):
        for d in range(1, GROUPS):
            page_copy(k, d).wait_recv()
        own_pages(k).wait()

        @pl.loop(0, PAGES // 4)
        def _(j):
            for i in range(4):
                rows = pl.ds(pl.multiple_of((j * 4 + i) * PAGE, PAGE), PAGE)
                cuts[k][rows, :] = recvs[k][idxs[0, j * 4 + i]]

        if k:
            near_copy(k).start()

    for k in range(1, COLS):
        q_copy(k).wait_recv()
        ring_copy(0, k, True).start()
        ring_copy(0, k, False).start()
    for s in range(1, 5):
        for k in range(COLS):
            ring_copy(s - 1, k, True).wait_recv()
            if s < 4:
                ring_copy(s, k, True).start()
            if s < 4:
                ring_copy(s - 1, k, False).wait_recv()
            if s < 3:
                ring_copy(s, k, False).start()
        if s == 2:
            compact(1)

    def queries(zb, c):
        part = qbuf[pl.ds(zb * COLS + 2 * c, 2), 0:RATIO]
        return part.reshape(HALF, HEAD)

    for b in range(COLS):
        rows = slice(KEYS + b * TOKENS, KEYS + (b + 1) * TOKENS)
        kc[rows, :] = qbuf[z * COLS + b, RATIO]
    kc[KEYS + COLS * TOKENS :, :] = jnp.zeros((HEAD - COLS * TOKENS, HEAD), BF16)
    suffix_v = [qbuf[z * COLS + b, RATIO + 1].astype(F32) for b in range(COLS)]
    suffix_v = jnp.concatenate(suffix_v + [jnp.zeros((HEAD - COLS * TOKENS, HEAD), F32)], axis=0)
    vt[0:HEAD, KEYS:] = suffix_v.T.astype(BF16)
    vt[HEAD:, KEYS:] = jnp.ones((SUMROWS, HEAD), BF16)

    shared_key = qbuf[0, RATIO][0:1, :].astype(F32)

    def prepare(k):
        base = (z * COLS + rot(x + COLS - k, COLS)) * KEYS
        for b in range(KEYS // HEAD):
            rows = slice(b * HEAD, (b + 1) * HEAD)
            token = base + b * HEAD + lax.broadcasted_iota(jnp.int32, (HEAD, HEAD), 0)
            seen = token < limit
            keys = nears[k][rows, 0:HEAD].astype(F32)
            values = nears[k][rows, HEAD:].astype(F32)
            kc[rows, :] = jnp.where(seen, keys, shared_key).astype(BF16)
            vt[0:HEAD, rows] = jnp.where(seen, values, 0.0).T.astype(BF16)
        lane = base + lax.broadcasted_iota(jnp.int32, (SUMROWS, KEYS), 1)
        vt[HEAD:, 0:KEYS] = jnp.where(lane < limit, 1.0, 0.0).astype(BF16)

    def scores(dst, peak, zb, c, first):
        size = WIDE if first else KEYS
        s = lax.dot_general(
            kc[0:size, :], queries(zb, c), (((1,), (1,)), ((), ())), preferred_element_type=F32
        )
        if first:
            key_row = lax.broadcasted_iota(jnp.int32, (HEAD, HALF), 0)
            column = lax.broadcasted_iota(jnp.int32, (HEAD, HALF), 1)
            asker = zb * (COLS * TOKENS) + (column // HEAD + 2 * c) * TOKENS + (column & (TOKENS - 1))
            seen = (key_row < COLS * TOKENS) & (z * (COLS * TOKENS) + key_row <= asker)
            own = jnp.where(seen, s[KEYS:], FLOOR)
            dst[KEYS:, :] = own
            s = s[0:KEYS]
        dst[0:KEYS, :] = s
        top = jnp.max(s, axis=0, keepdims=True)
        if first:
            top = jnp.maximum(top, jnp.max(own, axis=0, keepdims=True))
        peak[0:1, :] = jnp.ceil(top * 0.25) * 4.0

    def finish(src, peak, zb, c, first):
        size = WIDE if first else KEYS
        at = slice(c * HALF, (c + 1) * HALF)
        top = peak[0:1, :]
        if not first:
            before = mref[zb, 0:1, at]
            top = jnp.maximum(before, top)
        p = jnp.exp2(src[0:size, :] - top).astype(BF16)
        fresh = jnp.dot(vt[:, 0:size], p, preferred_element_type=F32)
        if not first:
            fresh = oacc[zb, :, at] * jnp.exp2(before - top) + fresh
        oacc[zb, :, at] = fresh
        mref[zb, 0:1, at] = top

    def attend(k, first):
        if k:
            near_copy(k).wait_recv()
        prepare(k)
        scores(sa, pa, 0, 0, first)

        @pl.loop(0, ROWS)
        def _(zb):
            scores(sb, pb, zb, 1, first)
            finish(sa, pa, zb, 0, first)
            scores(sa, pa, jnp.minimum(zb + 1, ROWS - 1), 0, first)
            finish(sb, pb, zb, 1, first)

    def sum_copy(s, q, up):
        block = rot(z + 4 - s, ROWS) if up else rot(z + 5 + s, ROWS)
        return pltpu.make_async_remote_copy(
            src_ref=osend.at[block, q], dst_ref=(upin if up else dnin).at[s, q],
            send_sem=(uosend if up else dosend).at[s, q],
            recv_sem=(uorecv if up else dorecv).at[s, q],
            device_id=(g, up_z if up else down_z, x), device_id_type=MESH,
        )

    def own_part(zb, q):
        at = slice(q * HEAD, (q + 1) * HEAD)
        return oacc[zb, 0:HEAD, at], mref[zb, 0:1, at], oacc[zb, HEAD : HEAD + 1, at]

    def join(part, arrived):
        o, m, l = part
        tile = arrived[HEAD:, :].astype(F32)
        m_in = tile[0:1]
        l_in = tile[1:2] + tile[2:3]
        top = jnp.maximum(m, m_in)
        mul, mul_in = jnp.exp2(m - top), jnp.exp2(m_in - top)
        return o * mul + arrived[0:HEAD, :].astype(F32) * mul_in, top, l * mul + l_in * mul_in

    def pack(zb, q, part):
        o, m, l = part
        l_high = l.astype(BF16).astype(F32)
        row = lax.broadcasted_iota(jnp.int32, (SUMROWS, HEAD), 0)
        tile = jnp.where(row == 0, m, jnp.where(row == 1, l_high, jnp.where(row == 2, l - l_high, 0.0)))
        osend[zb, q, 0:HEAD, :] = o.astype(BF16)
        osend[zb, q, HEAD:, :] = tile.astype(BF16)

    def relay(s, up):
        block = rot(z + 4 - s, ROWS) if up else rot(z + 5 + s, ROWS)
        for q in range(COLS):
            part = own_part(block, q)
            if s:
                sum_copy(s - 1, q, up).wait_recv()
                part = join(part, (upin if up else dnin).at[s - 1, q])
            pack(block, q, part)
            sum_copy(s, q, up).start()

    def f_copy(q, k):
        return pltpu.make_async_remote_copy(
            src_ref=fsend.at[q], dst_ref=frecv.at[x], send_sem=fsem.at[k], recv_sem=frsem.at[k],
            device_id=(g, z, q), device_id_type=MESH,
        )

    compact(2)
    attend(1, True)
    compact(3)
    attend(2, False)
    attend(3, False)
    compact(0)
    prepare(0)

    def block_at(n):
        return rot(z + LAST[n], ROWS)

    scores(sa, pa, block_at(0), 0, False)
    for n in range(ROWS):
        scores(sb, pb, block_at(n), 1, False)
        finish(sa, pa, block_at(n), 0, False)
        if n < ROWS - 1:
            scores(sa, pa, block_at(n + 1), 0, False)
        finish(sb, pb, block_at(n), 1, False)
        if n == 0:
            relay(0, True)
        if n == 1:
            relay(0, False)
        if n in (3, 5):
            relay(n // 2, True)
            relay(n // 2, False)
    relay(3, True)

    for q in range(COLS):
        part = own_part(z, q)
        sum_copy(2, q, False).wait_recv()
        part = join(part, dnin.at[2, q])
        sum_copy(3, q, True).wait_recv()
        o, m, l = join(part, upin.at[3, q])
        fsend[q] = (o / l).T.astype(BF16).reshape(RATIO, TOKENS, HEAD)
        k = rot(q + COLS - x, COLS)

        @pl.when(k > 0)
        def _():
            f_copy(q, k).start()

    frecv[x] = fsend[x]
    for k in range(1, COLS):
        f_copy(rot(x + k, COLS), k).wait_recv()
    for h in range(COLS):
        for i in range(RATIO):
            at = (h * RATIO + i) * HEAD
            out[:, at : at + HEAD] = frecv[h, i]

    for d in range(1, GROUPS):
        req_copy(d).wait_send()
    for k in range(1, COLS):
        q_copy(k).wait_send()
        near_copy(k).wait_send()
        f_copy(rot(x + k, COLS), k).wait_send()
    for s in range(4):
        for k in range(COLS):
            ring_copy(s, k, True).wait_send()
            sum_copy(s, k, True).wait_send()
            if s < 3:
                ring_copy(s, k, False).wait_send()
                sum_copy(s, k, False).wait_send()
    for k in range(COLS):
        for d in range(1, GROUPS):
            page_copy(k, d).wait_send()


def shards(
    query_raw, suffix_keyval, query_gain, key_norm_gain, positions, prefix_length,
    page_owner, page_slot, cache_pool,
):
    half = HEAD // 2
    frequency = 1000000.0 ** (-(2.0 / HEAD) * jnp.arange(half, dtype=F32))
    angles = positions[0].astype(F32)[:, None] * frequency[None, :]
    cosine, sine = jnp.cos(angles), jnp.sin(angles)
    cs = jnp.stack(
        [jnp.concatenate([cosine, cosine], axis=1), jnp.concatenate([-sine, sine], axis=1)]
    )
    owner = page_owner[0, :, 0]
    slot = page_slot[0]
    order = jnp.arange(PAGES, dtype=jnp.int32)
    same = (owner[:, None] == owner[None, :]) & (order[None, :] < order[:, None])
    place = owner * CAP + jnp.sum(same.astype(jnp.int32), axis=1)
    lanes = jnp.arange(HEAD, dtype=jnp.int32)
    wanted = jnp.where(
        lanes < CAP, jnp.arange(GROUPS, dtype=jnp.int32)[:, None] * CAP + lanes[None, :], -1
    )
    hit = wanted[:, :, None] == place[None, None, :]
    requests = jnp.sum(jnp.where(hit, slot[None, None, :], 0), axis=2)
    places = jnp.pad(place, (0, HEAD - PAGES))[None]
    tab = jnp.concatenate([requests, places], axis=0)
    tab = jnp.broadcast_to(tab[:, None, :], (GROUPS + 1, 8, HEAD))
    vmem = pl.BlockSpec(memory_space=pltpu.VMEM)
    page_half = (GROUPS * CAP, PAGE, 2 * HEAD)
    dma = pltpu.SemaphoreType.DMA
    result = pl.pallas_call(
        kernel,
        out_shape=jax.ShapeDtypeStruct((TOKENS, COLS * RATIO * HEAD), BF16),
        in_specs=[vmem] * 6
        + [pl.BlockSpec(memory_space=pltpu.SMEM), pl.BlockSpec(memory_space=pl.ANY)],
        out_specs=vmem,
        scratch_shapes=[pltpu.VMEM((POOL, PAGE, 2 * COLS * HEAD), BF16)]
        + [pltpu.VMEM(page_half, BF16)] * 8
        + [pltpu.VMEM((KEYS, 2 * HEAD), BF16)] * 7
        + [
            pltpu.VMEM((WIDE, HEAD), BF16),
            pltpu.VMEM((HEAD + SUMROWS, WIDE), BF16),
            pltpu.VMEM((WIDE, HALF), F32),
            pltpu.VMEM((WIDE, HALF), F32),
            pltpu.VMEM((8, HALF), F32),
            pltpu.VMEM((8, HALF), F32),
            pltpu.VMEM((COLS, RATIO + 2, TOKENS, HEAD), BF16),
            pltpu.VMEM((ROWS * COLS, RATIO + 2, TOKENS, HEAD), BF16),
            pltpu.VMEM((ROWS, HEAD + SUMROWS, BLOCK), F32),
            pltpu.VMEM((ROWS, 8, BLOCK), F32),
            pltpu.VMEM((ROWS, COLS, HEAD + SUMROWS, HEAD), BF16),
            pltpu.VMEM((4, COLS, HEAD + SUMROWS, HEAD), BF16),
            pltpu.VMEM((3, COLS, HEAD + SUMROWS, HEAD), BF16),
            pltpu.VMEM((COLS, RATIO, TOKENS, HEAD), BF16),
            pltpu.VMEM((COLS, RATIO, TOKENS, HEAD), BF16),
            pltpu.VMEM((GROUPS, 8, HEAD), jnp.int32),
            pltpu.SMEM((GROUPS, 8, HEAD), jnp.int32),
            pltpu.SMEM((8, HEAD), jnp.int32),
            dma((COLS, GROUPS)), dma((COLS, GROUPS)), dma((COLS + 1,)),
            dma((GROUPS,)), dma((GROUPS,)), dma((GROUPS + 1,)),
            dma((COLS,)), dma((COLS,)),
            dma((4, COLS)), dma((4, COLS)), dma((3, COLS)), dma((3, COLS)),
            dma((COLS,)), dma((COLS,)),
            dma((4, COLS)), dma((4, COLS)), dma((3, COLS)), dma((3, COLS)),
            dma((COLS,)), dma((COLS,)),
        ],
        compiler_params=pltpu.CompilerParams(
            collective_id=0, has_side_effects=True, vmem_limit_bytes=60 * 1024 * 1024
        ),
        name="spanned",
    )(
        tab, cs, query_raw[0], suffix_keyval[0], query_gain[None], key_norm_gain[None],
        prefix_length, cache_pool[0],
    )
    return result[None]


def solution(mesh):
    finer = Mesh(mesh.devices.reshape(GROUPS, ROWS, COLS), ("group", "ctx_0", "ctx_1"))
    ctx = ("ctx_0", "ctx_1")
    in_specs = (
        P("group", ctx, None),
        P("group", ctx, None),
        P(),
        P(),
        P("group", ctx),
        P("group"),
        P("group", ctx, None),
        P("group", ctx),
        P("group", ctx, None, None),
    )
    return jax.shard_map(
        shards, mesh=finer, in_specs=in_specs, out_specs=P("group", ctx, None), check_vma=False
    )
```

time: 126 us -> 90 us (0.71)
  the two profiles are of different devices: /device:TPU:1 before, /device:TPU:8 now
where the time goes in v2:
time: 90 us; the launch traced here: 89.9 us
  Pallas kernels  83.1 us (92%)
  other arithmetic  3.88 us (4%)
  local copies, waits for them, and re-layouts  2.19 us (2%)
    pallas_call x1, Pallas kernels, shards(): pl.pallas_call(kernel, out_shape=jax.ShapeDtypeStruct((TOKENS, COLS * RAT...  83.1 us

profile of v2, /device:TPU:8, one launch (start us, length us, event | category | flops | bytes accessed | tf_op | source)
XLA Modules:
  0.0 89.9 jit_solution(1678476893121859308)
XLA Ops:
  0.7 0.7 convert_bitcast_fusion
  1.3 0.9 %convert_reduce_fusion = s32[48]{0:T(128)S(1)} fusion(s32[48]{0:T(128)} %bitcast.24), kind=kLoop, calls=%fused_computation.1 | loop fusion | flops 11472 | bytes 384 | tf_op jit(solution)/shard_map/reduce_sum | solution.py:413
  2.2 0.7 multiply_add_fusion
  2.9 0.1 add_select_fusion
  3.0 0.7 select_reduce_fusion
  3.8 0.1 multiply_cosine_fusion
  3.9 0.1 maximum_bitcast_fusion
  4.0 0.6 pad_maximum_fusion.cs
  4.6 0.6 broadcast_in_dim.54.tab
  5.2 83.1 %spanned.1 = bf16[16,4096]{1,0:T(8,128)(2,1)} custom-call(s32[9,8,128]{2,1,0:T(8,128)} %broadcast_in_dim.54.tab, f32[2,16,128]{2,1,0:T(8,128)} %pad_maximum_fusion.cs, bf16[16,4096]{1,0:T(8,128)(2,1)} %bitcast.19, bf16[16,1024]{1,0:T(8,128)(2,1)} %bitcast.20, f32[1,128]{1,0:T(1,128)} %bitcast.22, f32[1,128]{1,0:T(1,128)} %bitcast.23, s32[1]{0:T(128)S(6)} %copy.11.plen, ...), custom_call_target="tpu_custom_call" | custom-call | tf_op jit(solution)/shard_map/spanned/pallas_call | solution.py:426
  88.3 1.6 %copy.12 = bf16[1,16,4096]{2,1,0:T(8,128)(2,1)} copy(bf16[1,16,4096]{2,1,0:T(8,128)(2,1)} %bitcast.18) | data formatting | bytes 262144
  (5 shorter events, 0.0 us)

commit v3 on v2

v3 whole, which is shorter than its diff:
```python
import jax
import jax.numpy as jnp
import numpy as np
from jax import lax
from jax.experimental import pallas as pl
from jax.experimental.pallas import tpu as pltpu
from jax.sharding import Mesh
from jax.sharding import PartitionSpec as P

MESH = pl.DeviceIdType.MESH
EPS = 1e-06
FLOOR = -65536.0
GROUPS = 8
ROWS = 8
COLS = 4
CAP = 12
PAGES = 48
POOL = 96
PAGE = 16
HEAD = 128
TOKENS = 16
RATIO = 8
KEYS = PAGES * PAGE
BLOCK = COLS * RATIO * TOKENS
HALF = BLOCK // 2
SUMROWS = 16
WIDE = KEYS + HEAD
CUT = 384
LAST = (4, 3, 5, 2, 6, 1, 7, 0)
QUARTERS = (2, 1, 3, 0)
FIRST_UP = (0, 1)
FIRST_DOWN = (2, 3)
F32 = jnp.float32
BF16 = jnp.bfloat16


def rot(a, n):
    return lax.rem(a, jnp.int32(n))


def kernel(
    owner, slots, freq, qraw_any, skv_any, qgain, kgain, plen, pool_any, out,
    qraw, skv, mix, tab, pool, send0, send1, send2, send3, recv0, recv1, recv2, recv3,
    near0, near1, near2, near3, cut1, cut2, cut3,
    kc, vt, sa, sb, pa, pb, qsend, qbuf, oacc, mref, osend, upin, dnin, fsend, frecv,
    reqv, reqs,
    psend, precv, lsem, rsend, rrecv, ssem, xsend, xrecv,
    upsend, uprecv, dnsend, dnrecv, nsend, nrecv, uosend, uorecv, dosend, dorecv, fsem, frsem,
):
    g = lax.axis_index("group")
    z = lax.axis_index("ctx_0")
    x = lax.axis_index("ctx_1")
    sends = (send0, send1, send2, send3)
    recvs = (recv0, recv1, recv2, recv3)
    nears = (near0, near1, near2, near3)
    cuts = (near0, cut1, cut2, cut3)
    limit = plen[0]
    turn = 1 + 2 * rot(g, 2)
    up_z, down_z = rot(z + 1, ROWS), rot(z + ROWS - 1, ROWS)

    load_q = pltpu.make_async_copy(qraw_any, qraw, lsem.at[COLS + 1])
    load_kv = pltpu.make_async_copy(skv_any, skv, lsem.at[COLS + 2])
    load_pool = pltpu.make_async_copy(pool_any, pool, lsem.at[COLS])
    load_q.start()
    load_kv.start()
    load_pool.start()
    barrier = pltpu.get_barrier_semaphore()
    partners = [(rot(g + n, GROUPS), z, x) for n in range(1, GROUPS)]
    partners += [(g, z, rot(x + n, COLS)) for n in range(1, COLS)]
    partners += [(g, up_z, x), (g, down_z, x)]
    for to in partners:
        pl.semaphore_signal(barrier, inc=1, device_id=to, device_id_type=MESH)

    mix[...] = jnp.full((8, HEAD), -1, jnp.int32)
    mix[0:1, 0:PAGES] = owner[...]
    mix[1:2, 0:PAGES] = slots[...]
    lane = lax.broadcasted_iota(jnp.int32, (HEAD, HEAD), 1)
    line = lax.broadcasted_iota(jnp.int32, (HEAD, HEAD), 0)
    owners = jnp.broadcast_to(mix[0:1, :], (HEAD, HEAD))
    earlier = (owners == owners.T) & (line < lane)
    rank = jnp.sum(jnp.where(earlier, 1, 0), axis=0, keepdims=True)
    place = mix[0:1, :] * CAP + rank
    places = jnp.broadcast_to(place, (HEAD, HEAD)).T
    named = jnp.broadcast_to(mix[1:2, :], (HEAD, HEAD)).T
    wanted = (places == lane) & (line < PAGES)
    tab[0:1, :] = jnp.sum(jnp.where(wanted, named, 0), axis=0, keepdims=True)
    tab[1:2, :] = place
    tab[2:8, :] = jnp.zeros((6, HEAD), jnp.int32)

    token_at = limit + (z * COLS + x) * TOKENS + lax.broadcasted_iota(jnp.int32, (TOKENS, HEAD), 0)
    angles = token_at.astype(F32) * freq[...]
    cosf = jnp.cos(angles)
    sinf = jnp.sin(angles)
    upper = lax.broadcasted_iota(jnp.int32, (TOKENS, HEAD), 1) >= HEAD // 2
    sinf = jnp.where(upper, sinf, -sinf)
    scale = HEAD ** (-0.5) * 1.4426950408889634

    def turned(raw, gain):
        raw = raw.astype(F32)
        mean = jnp.mean(raw * raw, axis=-1, keepdims=True)
        flat = raw * lax.rsqrt(mean + EPS) * gain
        return flat * cosf + pltpu.roll(flat, HEAD // 2, 1) * sinf

    load_q.wait()
    load_kv.wait()
    for i in range(COLS * RATIO):
        part = turned(qraw[:, i * HEAD : (i + 1) * HEAD], qgain[...])
        qsend[i // RATIO, i % RATIO] = (part * scale).astype(BF16)
    for i in range(COLS):
        part = turned(skv[:, i * HEAD : (i + 1) * HEAD], kgain[...])
        qsend[i, RATIO] = part.astype(BF16)
        qsend[i, RATIO + 1] = skv[:, (COLS + i) * HEAD : (COLS + i + 1) * HEAD]

    pl.semaphore_wait(barrier, len(partners))

    def req_copy(d):
        to = rot(g + d, GROUPS)
        return pltpu.make_async_remote_copy(
            src_ref=tab, dst_ref=reqv.at[g], send_sem=rsend.at[d], recv_sem=rrecv.at[d],
            device_id=(to, z, x), device_id_type=MESH,
        )

    mine = z * COLS + x

    def q_copy(k):
        to = rot(x + k, COLS)
        return pltpu.make_async_remote_copy(
            src_ref=qsend.at[to], dst_ref=qbuf.at[mine], send_sem=xsend.at[k], recv_sem=xrecv.at[k],
            device_id=(g, z, to), device_id_type=MESH,
        )

    for d in range(1, GROUPS):
        req_copy(d).start()
    for k in range(1, COLS):
        q_copy(k).start()

    def ring_copy(s, k, up):
        col = rot(x + COLS - k, COLS)
        away = rot(z + ROWS - s, ROWS) if up else rot(z + s, ROWS)
        place = away * COLS + col
        if s == 0 and k == 0:
            src = qsend.at[x, pl.ds(0, RATIO + 1)]
        else:
            src = qbuf.at[place, pl.ds(0, RATIO + 1)]
        return pltpu.make_async_remote_copy(
            src_ref=src, dst_ref=qbuf.at[place, pl.ds(0, RATIO + 1)],
            send_sem=(upsend if up else dnsend).at[s, k],
            recv_sem=(uprecv if up else dnrecv).at[s, k],
            device_id=(g, up_z if up else down_z, x), device_id_type=MESH,
        )

    ring_copy(0, 0, True).start()
    ring_copy(0, 0, False).start()
    qbuf[mine] = qsend[x]

    own_req = pltpu.make_async_copy(tab, reqs.at[g], ssem.at[0])
    own_req.start()

    def req_local(d):
        frm = rot(g + GROUPS - d, GROUPS)
        return pltpu.make_async_copy(reqv.at[frm], reqs.at[frm], ssem.at[d])

    for d in range(1, GROUPS):
        req_copy(d).wait_recv()
        req_local(d).start()
    own_req.wait()
    for d in range(1, GROUPS):
        req_local(d).wait()
    load_pool.wait()

    def page_copy(k, d):
        to = rot(g + d, GROUPS)
        return pltpu.make_async_remote_copy(
            src_ref=sends[k].at[pl.ds(to * CAP, CAP)], dst_ref=recvs[k].at[pl.ds(g * CAP, CAP)],
            send_sem=psend.at[k, d], recv_sem=precv.at[k, d],
            device_id=(to, z, x), device_id_type=MESH,
        )

    def own_pages(k):
        own = pl.ds(g * CAP, CAP)
        return pltpu.make_async_copy(sends[k].at[own], recvs[k].at[own], lsem.at[k])

    def gather(k):
        @pl.loop(0, GROUPS)
        def _(d):
            to = rot(g + d, GROUPS)
            head = rot(x + k * (1 + 2 * rot(to, 2)), COLS)
            key_at = pl.multiple_of(head * HEAD, HEAD)
            value_at = pl.multiple_of((COLS + head) * HEAD, HEAD)
            for r in range(CAP):
                slot = reqs[to, 0, g * CAP + r]
                sends[k][to * CAP + r, :, 0:HEAD] = pool[slot, :, pl.ds(key_at, HEAD)]
                sends[k][to * CAP + r, :, HEAD : 2 * HEAD] = pool[slot, :, pl.ds(value_at, HEAD)]

            @pl.when(d > 0)
            def _():
                page_copy(k, d).start()

        own_pages(k).start()

    for k in (1, 2, 3, 0):
        gather(k)

    def near_copy(k):
        return pltpu.make_async_remote_copy(
            src_ref=cuts[k], dst_ref=nears[k], send_sem=nsend.at[k], recv_sem=nrecv.at[k],
            device_id=(g, z, rot(x + k * turn, COLS)), device_id_type=MESH,
        )

    def compact(k):
        for d in range(1, GROUPS):
            page_copy(k, d).wait_recv()
        own_pages(k).wait()

        @pl.loop(0, PAGES // 4)
        def _(j):
            for i in range(4):
                rows = pl.ds(pl.multiple_of((j * 4 + i) * PAGE, PAGE), PAGE)
                cuts[k][rows, :] = recvs[k][reqs[g, 1, j * 4 + i]]

        if k:
            near_copy(k).start()

    for k in range(1, COLS):
        q_copy(k).wait_recv()
        ring_copy(0, k, True).start()
        ring_copy(0, k, False).start()
    for s in range(1, 5):
        for k in range(COLS):
            if s < 4 or k in FIRST_UP:
                ring_copy(s - 1, k, True).wait_recv()
            if s < 3 or (s == 3 and k in FIRST_UP):
                ring_copy(s, k, True).start()
            if s < 4 or k in FIRST_DOWN:
                ring_copy(s - 1, k, False).wait_recv()
            if s < 3 or (s == 3 and k in FIRST_DOWN):
                ring_copy(s, k, False).start()
        if s == 2:
            compact(1)

    def queries(zb, c):
        part = qbuf[pl.ds(zb * COLS + 2 * c, 2), 0:RATIO]
        return part.reshape(HALF, HEAD)

    for b in range(COLS):
        rows = slice(KEYS + b * TOKENS, KEYS + (b + 1) * TOKENS)
        kc[rows, :] = qbuf[z * COLS + b, RATIO]
    kc[KEYS + COLS * TOKENS :, :] = jnp.zeros((HEAD - COLS * TOKENS, HEAD), BF16)
    suffix_v = [qbuf[z * COLS + b, RATIO + 1].astype(F32) for b in range(COLS)]
    suffix_v = jnp.concatenate(suffix_v + [jnp.zeros((HEAD - COLS * TOKENS, HEAD), F32)], axis=0)
    vt[0:HEAD, KEYS:] = suffix_v.T.astype(BF16)
    vt[HEAD:, KEYS:] = jnp.ones((SUMROWS, HEAD), BF16)

    shared_key = qbuf[0, RATIO][0:1, :].astype(F32)

    def prepare(k):
        base = (z * COLS + rot(x + 3 * COLS - k * turn, COLS)) * KEYS
        for b in range(KEYS // HEAD):
            rows = slice(b * HEAD, (b + 1) * HEAD)
            token = base + b * HEAD + lax.broadcasted_iota(jnp.int32, (HEAD, HEAD), 0)
            seen = token < limit
            keys = nears[k][rows, 0:HEAD].astype(F32)
            values = nears[k][rows, HEAD:].astype(F32)
            kc[rows, :] = jnp.where(seen, keys, shared_key).astype(BF16)
            vt[0:HEAD, rows] = jnp.where(seen, values, 0.0).T.astype(BF16)
        lane = base + lax.broadcasted_iota(jnp.int32, (SUMROWS, KEYS), 1)
        vt[HEAD:, 0:KEYS] = jnp.where(lane < limit, 1.0, 0.0).astype(BF16)

    def scores(dst, peak, zb, c, first):
        step(None, None, 0, 0, dst, peak, zb, c, first)

    def finish(src, peak, zb, c, first):
        step(src, peak, zb, c, None, None, 0, 0, first)

    def step(src, src_peak, zb, c, dst, dst_peak, next_zb, next_c, first):
        size = WIDE if first else KEYS
        if src is not None:
            top = src_peak[0:1, :]
            if not first:
                before = jnp.concatenate([mref[zb, q, 0:1, :] for q in (2 * c, 2 * c + 1)], axis=1)
                top = jnp.maximum(before, top)
        if dst is not None:
            asked = queries(next_zb, next_c)
        weights, tops = [], []
        for lo in range(0, size, CUT):
            hi = min(lo + CUT, size)
            if dst is not None:
                s = lax.dot_general(
                    kc[lo:hi, :], asked, (((1,), (1,)), ((), ())), preferred_element_type=F32
                )
                if hi > KEYS:
                    key_row = lax.broadcasted_iota(jnp.int32, (hi - lo, HALF), 0) + (lo - KEYS)
                    column = lax.broadcasted_iota(jnp.int32, (hi - lo, HALF), 1)
                    asker = next_zb * (COLS * TOKENS) + (column // HEAD + 2 * next_c) * TOKENS
                    asker = asker + (column & (TOKENS - 1))
                    seen = (key_row < COLS * TOKENS) & (z * (COLS * TOKENS) + key_row <= asker)
                    s = jnp.where((key_row < 0) | seen, s, FLOOR)
                dst[lo:hi, :] = s
                tops.append(jnp.max(s, axis=0, keepdims=True))
            if src is not None:
                weights.append(jnp.exp2(src[lo:hi, :] - top).astype(BF16))
        if dst is not None:
            best = tops[0]
            for t in tops[1:]:
                best = jnp.maximum(best, t)
            dst_peak[0:1, :] = jnp.ceil(best * 0.25) * 4.0
        if src is not None:
            fresh = jnp.dot(vt[:, 0:size], jnp.concatenate(weights, axis=0), preferred_element_type=F32)
            for i in range(2):
                q, at = 2 * c + i, slice(i * HEAD, (i + 1) * HEAD)
                part = fresh[:, at]
                if not first:
                    part = oacc[zb, q] * jnp.exp2(before[:, at] - top[:, at]) + part
                oacc[zb, q] = part
                mref[zb, q, 0:1, :] = top[:, at]

    def attend(k, first):
        if k:
            near_copy(k).wait_recv()
        prepare(k)
        scores(sa, pa, 0, 0, first)

        @pl.loop(0, ROWS)
        def _(zb):
            step(sa, pa, zb, 0, sb, pb, zb, 1, first)
            step(sb, pb, zb, 1, sa, pa, jnp.minimum(zb + 1, ROWS - 1), 0, first)

    def quarter(j):
        return rot(x + QUARTERS[j], COLS)

    def sum_copy(s, j, up):
        block = rot(z + 4 - s, ROWS) if up else rot(z + 4 + s, ROWS)
        return pltpu.make_async_remote_copy(
            src_ref=osend.at[block, quarter(j)], dst_ref=(upin if up else dnin).at[s, j],
            send_sem=(uosend if up else dosend).at[s, j],
            recv_sem=(uorecv if up else dorecv).at[s, j],
            device_id=(g, up_z if up else down_z, x), device_id_type=MESH,
        )

    def own_part(zb, q):
        return oacc[zb, q, 0:HEAD, :], mref[zb, q, 0:1, :], oacc[zb, q, HEAD : HEAD + 1, :]

    def join(part, arrived):
        o, m, l = part
        tile = arrived[HEAD:, :].astype(F32)
        m_in = tile[0:1]
        l_in = tile[1:2] + tile[2:3]
        top = jnp.maximum(m, m_in)
        mul, mul_in = jnp.exp2(m - top), jnp.exp2(m_in - top)
        return o * mul + arrived[0:HEAD, :].astype(F32) * mul_in, top, l * mul + l_in * mul_in

    def pack(zb, q, part):
        o, m, l = part
        l_high = l.astype(BF16).astype(F32)
        row = lax.broadcasted_iota(jnp.int32, (SUMROWS, HEAD), 0)
        tile = jnp.where(row == 0, m, jnp.where(row == 1, l_high, jnp.where(row == 2, l - l_high, 0.0)))
        osend[zb, q, 0:HEAD, :] = o.astype(BF16)
        osend[zb, q, HEAD:, :] = tile.astype(BF16)

    def relay(s, early, late):
        for js in zip(early, late):
            for up, j in zip((True, False), js):
                block = rot(z + 4 - s, ROWS) if up else rot(z + 4 + s, ROWS)
                q = quarter(j)
                part = own_part(block, q)
                if s > 1 or (s == 1 and j in (FIRST_UP if up else FIRST_DOWN)):
                    sum_copy(s - 1, j, up).wait_recv()
                    part = join(part, (upin if up else dnin).at[s - 1, j])
                pack(block, q, part)
                sum_copy(s, j, up).start()

    def f_copy(q, k):
        return pltpu.make_async_remote_copy(
            src_ref=fsend.at[q], dst_ref=frecv.at[x], send_sem=fsem.at[k], recv_sem=frsem.at[k],
            device_id=(g, z, q), device_id_type=MESH,
        )

    compact(2)
    attend(1, True)
    compact(3)
    attend(2, False)
    attend(3, False)
    compact(0)
    prepare(0)

    def block_at(n):
        return rot(z + LAST[n], ROWS)

    scores(sa, pa, block_at(0), 0, False)
    for n in range(ROWS):
        step(sa, pa, block_at(n), 0, sb, pb, block_at(n), 1, False)
        if n < ROWS - 1:
            step(sb, pb, block_at(n), 1, sa, pa, block_at(n + 1), 0, False)
        else:
            finish(sb, pb, block_at(n), 1, False)
        if n == 0:
            relay(0, FIRST_UP, FIRST_DOWN)
        if n == 2:
            relay(1, FIRST_DOWN, FIRST_UP)
        if n == 4:
            relay(1, FIRST_UP, FIRST_DOWN)
        if n == 6:
            relay(2, FIRST_DOWN, FIRST_UP)
    relay(2, FIRST_UP, FIRST_DOWN)
    relay(3, FIRST_DOWN, FIRST_UP)
    relay(3, FIRST_UP, FIRST_DOWN)

    for j in range(COLS):
        q = quarter(j)
        part = own_part(z, q)
        sum_copy(3, j, False).wait_recv()
        part = join(part, dnin.at[3, j])
        sum_copy(3, j, True).wait_recv()
        o, m, l = join(part, upin.at[3, j])
        fsend[q] = (o / l).T.astype(BF16).reshape(RATIO, TOKENS, HEAD)
        if QUARTERS[j]:
            f_copy(q, QUARTERS[j]).start()

    frecv[x] = fsend[x]
    for k in range(1, COLS):
        f_copy(rot(x + k, COLS), k).wait_recv()
    for h in range(COLS):
        for i in range(RATIO):
            at = (h * RATIO + i) * HEAD
            out[:, at : at + HEAD] = frecv[h, i].astype(F32)

    for d in range(1, GROUPS):
        req_copy(d).wait_send()
    for k in range(1, COLS):
        q_copy(k).wait_send()
        near_copy(k).wait_send()
        f_copy(rot(x + k, COLS), k).wait_send()
    for s in range(4):
        for k in range(COLS):
            if s < 3 or k in FIRST_UP:
                ring_copy(s, k, True).wait_send()
            if s < 3 or k in FIRST_DOWN:
                ring_copy(s, k, False).wait_send()
            if s or k in FIRST_UP:
                sum_copy(s, k, True).wait_send()
            if s or k in FIRST_DOWN:
                sum_copy(s, k, False).wait_send()
    for k in range(COLS):
        for d in range(1, GROUPS):
            page_copy(k, d).wait_send()


def shards(
    query_raw, suffix_keyval, query_gain, key_norm_gain, positions, prefix_length,
    page_owner, page_slot, cache_pool,
):
    half = np.arange(HEAD) % (HEAD // 2)
    frequency = (1000000.0 ** (-(2.0 / HEAD) * half)).astype(np.float32)[None]
    vmem = pl.BlockSpec(memory_space=pltpu.VMEM)
    far = pl.BlockSpec(memory_space=pl.ANY)
    page_half = (GROUPS * CAP, PAGE, 2 * HEAD)
    dma = pltpu.SemaphoreType.DMA
    result = pl.pallas_call(
        kernel,
        out_shape=jax.ShapeDtypeStruct((TOKENS, COLS * RATIO * HEAD), F32),
        in_specs=[vmem] * 3 + [far] * 2 + [vmem] * 2 + [pl.BlockSpec(memory_space=pltpu.SMEM), far],
        out_specs=vmem,
        scratch_shapes=[
            pltpu.VMEM((TOKENS, COLS * RATIO * HEAD), BF16),
            pltpu.VMEM((TOKENS, 2 * COLS * HEAD), BF16),
            pltpu.VMEM((8, HEAD), jnp.int32),
            pltpu.VMEM((8, HEAD), jnp.int32),
        ]
        + [pltpu.VMEM((POOL, PAGE, 2 * COLS * HEAD), BF16)]
        + [pltpu.VMEM(page_half, BF16)] * 8
        + [pltpu.VMEM((KEYS, 2 * HEAD), BF16)] * 7
        + [
            pltpu.VMEM((WIDE, HEAD), BF16),
            pltpu.VMEM((HEAD + SUMROWS, WIDE), BF16),
            pltpu.VMEM((WIDE, HALF), F32),
            pltpu.VMEM((WIDE, HALF), F32),
            pltpu.VMEM((8, HALF), F32),
            pltpu.VMEM((8, HALF), F32),
            pltpu.VMEM((COLS, RATIO + 2, TOKENS, HEAD), BF16),
            pltpu.VMEM((ROWS * COLS, RATIO + 2, TOKENS, HEAD), BF16),
            pltpu.VMEM((ROWS, COLS, HEAD + SUMROWS, HEAD), F32),
            pltpu.VMEM((ROWS, COLS, 8, HEAD), F32),
            pltpu.VMEM((ROWS, COLS, HEAD + SUMROWS, HEAD), BF16),
            pltpu.VMEM((4, COLS, HEAD + SUMROWS, HEAD), BF16),
            pltpu.VMEM((4, COLS, HEAD + SUMROWS, HEAD), BF16),
            pltpu.VMEM((COLS, RATIO, TOKENS, HEAD), BF16),
            pltpu.VMEM((COLS, RATIO, TOKENS, HEAD), BF16),
            pltpu.VMEM((GROUPS, 8, HEAD), jnp.int32),
            pltpu.SMEM((GROUPS, 8, HEAD), jnp.int32),
            dma((COLS, GROUPS)), dma((COLS, GROUPS)), dma((COLS + 3,)),
            dma((GROUPS,)), dma((GROUPS,)), dma((GROUPS,)),
            dma((COLS,)), dma((COLS,)),
            dma((4, COLS)), dma((4, COLS)), dma((4, COLS)), dma((4, COLS)),
            dma((COLS,)), dma((COLS,)),
            dma((4, COLS)), dma((4, COLS)), dma((4, COLS)), dma((4, COLS)),
            dma((COLS,)), dma((COLS,)),
        ],
        compiler_params=pltpu.CompilerParams(
            collective_id=0, has_side_effects=True, vmem_limit_bytes=60 * 1024 * 1024
        ),
        name="spanned",
    )(
        page_owner.reshape(1, PAGES), page_slot, jnp.asarray(frequency), query_raw[0],
        suffix_keyval[0], query_gain[None], key_norm_gain[None], prefix_length, cache_pool[0],
    )
    return result.astype(BF16)[None]


def solution(mesh):
    finer = Mesh(mesh.devices.reshape(GROUPS, ROWS, COLS), ("group", "ctx_0", "ctx_1"))
    ctx = ("ctx_0", "ctx_1")
    in_specs = (
        P("group", ctx, None),
        P("group", ctx, None),
        P(),
        P(),
        P("group", ctx),
        P("group"),
        P("group", ctx, None),
        P("group", ctx),
        P("group", ctx, None, None),
    )
    return jax.shard_map(
        shards, mesh=finer, in_specs=in_specs, out_specs=P("group", ctx, None), check_vma=False
    )
```

time: 90 us -> 80.3 us (0.89)
  the two profiles are of different devices: /device:TPU:8 before, /device:TPU:1 now
where the time goes in v3:
time: 80.3 us; the launch traced here: 79.6 us
  Pallas kernels  77.3 us (96%)
  other arithmetic  1.62 us (2%)
    pallas_call x1, Pallas kernels, shards(): pl.pallas_call(kernel, out_shape=jax.ShapeDtypeStruct((TOKENS, COLS * RAT...  77.3 us
    broadcast_in_dim x1, other arithmetic, shards(): return result.astype(BF16)[None]  1.62 us

profile of v3, /device:TPU:1, one launch (start us, length us, event | category | flops | bytes accessed | tf_op | source)
XLA Modules:
  0.0 79.6 jit_solution(7737562101064711569)
XLA Ops:
  0.7 77.3 %spanned.1 = f32[16,4096]{1,0:T(8,128)} custom-call(s32[1,48]{1,0:T(1,128)} %bitcast.11, s32[1,48]{1,0:T(1,128)} %slots.1, f32[1,128]{1,0:T(1,128)} %constant.2.clone.freq, bf16[16,4096]{1,0:T(8,128)(2,1)} %bitcast.9, bf16[16,1024]{1,0:T(8,128)(2,1)} %bitcast.10, f32[1,128]{1,0:T(1,128)} %bitcast.12, f32[1,128]{1,0:T(1,128)} %bitcast.13, s32[1]{0:T(128)S(6)} %copy.10.plen, ...), custom_call_target="tpu_custom_call" | custom-call | tf_op jit(solution)/shard_map/spanned/pallas_call | solution.py:458
  77.9 1.6 %convert_bitcast_fusion = bf16[1,16,4096]{2,1,0:T(8,128)(2,1)} fusion(f32[16,4096]{1,0:T(8,128)} %spanned.1), kind=kLoop, calls=%fused_computation | loop fusion | flops 65536 | bytes 393216 | tf_op jit(solution)/shard_map/broadcast_in_dim | solution.py:506

commit v4 on v3

--- a/solution.py
+++ b/solution.py
@@ -23,7 +23,7 @@
 KEYS = PAGES * PAGE
 BLOCK = COLS * RATIO * TOKENS
 HALF = BLOCK // 2
-SUMROWS = 16
+SUMROWS = 8
 WIDE = KEYS + HEAD
 CUT = 384
 LAST = (4, 3, 5, 2, 6, 1, 7, 0)
@@ -42,7 +42,7 @@
     owner, slots, freq, qraw_any, skv_any, qgain, kgain, plen, pool_any, out,
     qraw, skv, mix, tab, pool, send0, send1, send2, send3, recv0, recv1, recv2, recv3,
     near0, near1, near2, near3, cut1, cut2, cut3,
-    kc, vt, sa, sb, pa, pb, qsend, qbuf, oacc, mref, osend, upin, dnin, fsend, frecv,
+    kc, vt, sa, sb, pa, pb, qsend, qbuf, oacc, mref, osend, upin, dnin, upend, dnend, ownend,
     reqv, reqs,
     psend, precv, lsem, rsend, rrecv, ssem, xsend, xrecv,
     upsend, uprecv, dnsend, dnrecv, nsend, nrecv, uosend, uorecv, dosend, dorecv, fsem, frsem,
@@ -67,7 +67,7 @@
     barrier = pltpu.get_barrier_semaphore()
     partners = [(rot(g + n, GROUPS), z, x) for n in range(1, GROUPS)]
     partners += [(g, z, rot(x + n, COLS)) for n in range(1, COLS)]
-    partners += [(g, up_z, x), (g, down_z, x)]
+    partners += [(g, to_z, rot(x + n, COLS)) for n in range(COLS) for to_z in (up_z, down_z)]
     for to in partners:
         pl.semaphore_signal(barrier, inc=1, device_id=to, device_id_type=MESH)
 
@@ -330,11 +330,22 @@
 
     def sum_copy(s, j, up):
         block = rot(z + 4 - s, ROWS) if up else rot(z + 4 + s, ROWS)
-        return pltpu.make_async_remote_copy(
-            src_ref=osend.at[block, quarter(j)], dst_ref=(upin if up else dnin).at[s, j],
+        if s < 3:
+            dst, to_x = (upin if up else dnin).at[s, j], x
+        else:
+            dst, to_x = (upend if up else dnend).at[x], quarter(j)
+        return pltpu.make_async_remote_copy(
+            src_ref=osend.at[block, quarter(j)], dst_ref=dst,
             send_sem=(uosend if up else dosend).at[s, j],
             recv_sem=(uorecv if up else dorecv).at[s, j],
-            device_id=(g, up_z if up else down_z, x), device_id_type=MESH,
+            device_id=(g, up_z if up else down_z, to_x), device_id_type=MESH,
+        )
+
+    def own_copy(j):
+        return pltpu.make_async_remote_copy(
+            src_ref=osend.at[z, quarter(j)], dst_ref=ownend.at[x],
+            send_sem=fsem.at[j], recv_sem=frsem.at[j],
+            device_id=(g, z, quarter(j)), device_id_type=MESH,
         )
 
     def own_part(zb, q):
@@ -368,12 +379,6 @@
                     part = join(part, (upin if up else dnin).at[s - 1, j])
                 pack(block, q, part)
                 sum_copy(s, j, up).start()
-
-    def f_copy(q, k):
-        return pltpu.make_async_remote_copy(
-            src_ref=fsend.at[q], dst_ref=frecv.at[x], send_sem=fsem.at[k], recv_sem=frsem.at[k],
-            device_id=(g, z, q), device_id_type=MESH,
-        )
 
     compact(2)
     attend(1, True)
@@ -401,35 +406,35 @@
             relay(1, FIRST_UP, FIRST_DOWN)
         if n == 6:
             relay(2, FIRST_DOWN, FIRST_UP)
+    for j in range(COLS):
+        pack(z, quarter(j), own_part(z, quarter(j)))
+        if QUARTERS[j]:
+            own_copy(j).start()
+    ownend[x] = osend[z, x]
     relay(2, FIRST_UP, FIRST_DOWN)
     relay(3, FIRST_DOWN, FIRST_UP)
     relay(3, FIRST_UP, FIRST_DOWN)
 
     for j in range(COLS):
-        q = quarter(j)
-        part = own_part(z, q)
+        if QUARTERS[j]:
+            own_copy(j).wait_recv()
         sum_copy(3, j, False).wait_recv()
-        part = join(part, dnin.at[3, j])
         sum_copy(3, j, True).wait_recv()
-        o, m, l = join(part, upin.at[3, j])
-        fsend[q] = (o / l).T.astype(BF16).reshape(RATIO, TOKENS, HEAD)
-        if QUARTERS[j]:
-            f_copy(q, QUARTERS[j]).start()
-
-    frecv[x] = fsend[x]
-    for k in range(1, COLS):
-        f_copy(rot(x + k, COLS), k).wait_recv()
     for h in range(COLS):
+        tile = ownend[h, HEAD:, :].astype(F32)
+        part = (ownend[h, 0:HEAD, :].astype(F32), tile[0:1], tile[1:2] + tile[2:3])
+        o, m, l = join(join(part, dnend.at[h]), upend.at[h])
+        rows = (o / l).T.astype(BF16).astype(F32)
         for i in range(RATIO):
             at = (h * RATIO + i) * HEAD
-            out[:, at : at + HEAD] = frecv[h, i].astype(F32)
+            out[:, at : at + HEAD] = rows[i * TOKENS : (i + 1) * TOKENS]
 
     for d in range(1, GROUPS):
         req_copy(d).wait_send()
     for k in range(1, COLS):
         q_copy(k).wait_send()
         near_copy(k).wait_send()
-        f_copy(rot(x + k, COLS), k).wait_send()
+        own_copy(k - 1).wait_send()
     for s in range(4):
         for k in range(COLS):
             if s < 3 or k in FIRST_UP:
@@ -481,10 +486,11 @@
             pltpu.VMEM((ROWS, COLS, HEAD + SUMROWS, HEAD), F32),
             pltpu.VMEM((ROWS, COLS, 8, HEAD), F32),
             pltpu.VMEM((ROWS, COLS, HEAD + SUMROWS, HEAD), BF16),
-            pltpu.VMEM((4, COLS, HEAD + SUMROWS, HEAD), BF16),
-            pltpu.VMEM((4, COLS, HEAD + SUMROWS, HEAD), BF16),
-            pltpu.VMEM((COLS, RATIO, TOKENS, HEAD), BF16),
-            pltpu.VMEM((COLS, RATIO, TOKENS, HEAD), BF16),
+            pltpu.VMEM((3, COLS, HEAD + SUMROWS, HEAD), BF16),
+            pltpu.VMEM((3, COLS, HEAD + SUMROWS, HEAD), BF16),
+            pltpu.VMEM((COLS, HEAD + SUMROWS, HEAD), BF16),
+            pltpu.VMEM((COLS, HEAD + SUMROWS, HEAD), BF16),
+            pltpu.VMEM((COLS, HEAD + SUMROWS, HEAD), BF16),
             pltpu.VMEM((GROUPS, 8, HEAD), jnp.int32),
             pltpu.SMEM((GROUPS, 8, HEAD), jnp.int32),
             dma((COLS, GROUPS)), dma((COLS, GROUPS)), dma((COLS + 3,)),

time: 80.3 us -> 77.5 us (0.965)
  Pallas kernels: 77.3 us -> 74.8 us
    pallas_call x1, Pallas kernels: 77.3 us -> 74.8 us  [shards(): pl.pallas_call(kernel, out_shape=jax.ShapeDtypeStruct((TOKENS, COLS * RAT...]
where the time goes in v4:
time: 77.5 us; the launch traced here: 77.1 us
  Pallas kernels  74.8 us (97%)
  other arithmetic  1.62 us (2%)
    pallas_call x1, Pallas kernels, shards(): pl.pallas_call(kernel, out_shape=jax.ShapeDtypeStruct((TOKENS, COLS * RAT...  74.8 us
    broadcast_in_dim x1, other arithmetic, shards(): return result.astype(BF16)[None]  1.62 us

profile of v4, /device:TPU:1, one launch (start us, length us, event | category | flops | bytes accessed | tf_op | source)
XLA Modules:
  0.0 77.1 jit_solution(6096187441534001551)
XLA Ops:
  0.7 74.8 %spanned.1 = f32[16,4096]{1,0:T(8,128)} custom-call(s32[1,48]{1,0:T(1,128)} %bitcast.11, s32[1,48]{1,0:T(1,128)} %slots.1, f32[1,128]{1,0:T(1,128)} %constant.2.clone.freq, bf16[16,4096]{1,0:T(8,128)(2,1)} %bitcast.9, bf16[16,1024]{1,0:T(8,128)(2,1)} %bitcast.10, f32[1,128]{1,0:T(1,128)} %bitcast.12, f32[1,128]{1,0:T(1,128)} %bitcast.13, s32[1]{0:T(128)S(6)} %copy.10.plen, ...), custom_call_target="tpu_custom_call" | custom-call | tf_op jit(solution)/shard_map/spanned/pallas_call | solution.py:463
  75.5 1.6 %convert_bitcast_fusion = bf16[1,16,4096]{2,1,0:T(8,128)(2,1)} fusion(f32[16,4096]{1,0:T(8,128)} %spanned.1), kind=kLoop, calls=%fused_computation | loop fusion | flops 65536 | bytes 393216 | tf_op jit(solution)/shard_map/broadcast_in_dim | solution.py:512

commit v5 on v4

--- a/solution.py
+++ b/solution.py
@@ -25,6 +25,7 @@
 HALF = BLOCK // 2
 SUMROWS = 8
 WIDE = KEYS + HEAD
+PAIR = 2 * KEYS
 CUT = 384
 LAST = (4, 3, 5, 2, 6, 1, 7, 0)
 QUARTERS = (2, 1, 3, 0)
@@ -43,7 +44,7 @@
     qraw, skv, mix, tab, pool, send0, send1, send2, send3, recv0, recv1, recv2, recv3,
     near0, near1, near2, near3, cut1, cut2, cut3,
     kc, vt, sa, sb, pa, pb, qsend, qbuf, oacc, mref, osend, upin, dnin, upend, dnend, ownend,
-    reqv, reqs,
+    reqs,
     psend, precv, lsem, rsend, rrecv, ssem, xsend, xrecv,
     upsend, uprecv, dnsend, dnrecv, nsend, nrecv, uosend, uorecv, dosend, dorecv, fsem, frsem,
 ):
@@ -116,7 +117,7 @@
     def req_copy(d):
         to = rot(g + d, GROUPS)
         return pltpu.make_async_remote_copy(
-            src_ref=tab, dst_ref=reqv.at[g], send_sem=rsend.at[d], recv_sem=rrecv.at[d],
+            src_ref=tab, dst_ref=reqs.at[g], send_sem=rsend.at[d], recv_sem=rrecv.at[d],
             device_id=(to, z, x), device_id_type=MESH,
         )
 
@@ -156,16 +157,9 @@
     own_req = pltpu.make_async_copy(tab, reqs.at[g], ssem.at[0])
     own_req.start()
 
-    def req_local(d):
-        frm = rot(g + GROUPS - d, GROUPS)
-        return pltpu.make_async_copy(reqv.at[frm], reqs.at[frm], ssem.at[d])
-
     for d in range(1, GROUPS):
         req_copy(d).wait_recv()
-        req_local(d).start()
     own_req.wait()
-    for d in range(1, GROUPS):
-        req_local(d).wait()
     load_pool.wait()
 
     def page_copy(k, d):
@@ -245,15 +239,15 @@
     for b in range(COLS):
         rows = slice(KEYS + b * TOKENS, KEYS + (b + 1) * TOKENS)
         kc[rows, :] = qbuf[z * COLS + b, RATIO]
-    kc[KEYS + COLS * TOKENS :, :] = jnp.zeros((HEAD - COLS * TOKENS, HEAD), BF16)
+    kc[KEYS + COLS * TOKENS : WIDE, :] = jnp.zeros((HEAD - COLS * TOKENS, HEAD), BF16)
     suffix_v = [qbuf[z * COLS + b, RATIO + 1].astype(F32) for b in range(COLS)]
     suffix_v = jnp.concatenate(suffix_v + [jnp.zeros((HEAD - COLS * TOKENS, HEAD), F32)], axis=0)
-    vt[0:HEAD, KEYS:] = suffix_v.T.astype(BF16)
-    vt[HEAD:, KEYS:] = jnp.ones((SUMROWS, HEAD), BF16)
+    vt[0:HEAD, KEYS:WIDE] = suffix_v.T.astype(BF16)
+    vt[HEAD:, KEYS:WIDE] = jnp.ones((SUMROWS, HEAD), BF16)
 
     shared_key = qbuf[0, RATIO][0:1, :].astype(F32)
 
-    def prepare(k):
+    def prepare(k, start=0):
         base = (z * COLS + rot(x + 3 * COLS - k * turn, COLS)) * KEYS
         for b in range(KEYS // HEAD):
             rows = slice(b * HEAD, (b + 1) * HEAD)
@@ -261,10 +255,11 @@
             seen = token < limit
             keys = nears[k][rows, 0:HEAD].astype(F32)
             values = nears[k][rows, HEAD:].astype(F32)
-            kc[rows, :] = jnp.where(seen, keys, shared_key).astype(BF16)
-            vt[0:HEAD, rows] = jnp.where(seen, values, 0.0).T.astype(BF16)
+            put = slice(start + b * HEAD, start + (b + 1) * HEAD)
+            kc[put, :] = jnp.where(seen, keys, shared_key).astype(BF16)
+            vt[0:HEAD, put] = jnp.where(seen, values, 0.0).T.astype(BF16)
         lane = base + lax.broadcasted_iota(jnp.int32, (SUMROWS, KEYS), 1)
-        vt[HEAD:, 0:KEYS] = jnp.where(lane < limit, 1.0, 0.0).astype(BF16)
+        vt[HEAD:, start : start + KEYS] = jnp.where(lane < limit, 1.0, 0.0).astype(BF16)
 
     def scores(dst, peak, zb, c, first):
         step(None, None, 0, 0, dst, peak, zb, c, first)
@@ -274,6 +269,7 @@
 
     def step(src, src_peak, zb, c, dst, dst_peak, next_zb, next_c, first):
         size = WIDE if first else KEYS
+        size = PAIR if first is None else size
         if src is not None:
             top = src_peak[0:1, :]
             if not first:
@@ -288,7 +284,7 @@
                 s = lax.dot_general(
                     kc[lo:hi, :], asked, (((1,), (1,)), ((), ())), preferred_element_type=F32
                 )
-                if hi > KEYS:
+                if first and hi > KEYS:
                     key_row = lax.broadcasted_iota(jnp.int32, (hi - lo, HALF), 0) + (lo - KEYS)
                     column = lax.broadcasted_iota(jnp.int32, (hi - lo, HALF), 1)
                     asker = next_zb * (COLS * TOKENS) + (column // HEAD + 2 * next_c) * TOKENS
@@ -384,34 +380,37 @@
     attend(1, True)
     compact(3)
     attend(2, False)
-    attend(3, False)
+
+    near_copy(3).wait_recv()
+    prepare(3)
     compact(0)
-    prepare(0)
+    prepare(0, KEYS)
 
     def block_at(n):
         return rot(z + LAST[n], ROWS)
 
-    scores(sa, pa, block_at(0), 0, False)
+    scores(sa, pa, block_at(0), 0, None)
     for n in range(ROWS):
-        step(sa, pa, block_at(n), 0, sb, pb, block_at(n), 1, False)
+        step(sa, pa, block_at(n), 0, sb, pb, block_at(n), 1, None)
         if n < ROWS - 1:
-            step(sb, pb, block_at(n), 1, sa, pa, block_at(n + 1), 0, False)
+            step(sb, pb, block_at(n), 1, sa, pa, block_at(n + 1), 0, None)
         else:
-            finish(sb, pb, block_at(n), 1, False)
+            finish(sb, pb, block_at(n), 1, None)
         if n == 0:
             relay(0, FIRST_UP, FIRST_DOWN)
         if n == 2:
             relay(1, FIRST_DOWN, FIRST_UP)
-        if n == 4:
+        if n == 3:
             relay(1, FIRST_UP, FIRST_DOWN)
+        if n == 5:
+            relay(2, FIRST_DOWN, FIRST_UP)
         if n == 6:
-            relay(2, FIRST_DOWN, FIRST_UP)
+            relay(2, FIRST_UP, FIRST_DOWN)
     for j in range(COLS):
         pack(z, quarter(j), own_part(z, quarter(j)))
         if QUARTERS[j]:
             own_copy(j).start()
     ownend[x] = osend[z, x]
-    relay(2, FIRST_UP, FIRST_DOWN)
     relay(3, FIRST_DOWN, FIRST_UP)
     relay(3, FIRST_UP, FIRST_DOWN)
 
@@ -475,10 +474,10 @@
         + [pltpu.VMEM(page_half, BF16)] * 8
         + [pltpu.VMEM((KEYS, 2 * HEAD), BF16)] * 7
         + [
-            pltpu.VMEM((WIDE, HEAD), BF16),
-            pltpu.VMEM((HEAD + SUMROWS, WIDE), BF16),
-            pltpu.VMEM((WIDE, HALF), F32),
-            pltpu.VMEM((WIDE, HALF), F32),
+            pltpu.VMEM((PAIR, HEAD), BF16),
+            pltpu.VMEM((HEAD + SUMROWS, PAIR), BF16),
+            pltpu.VMEM((PAIR, HALF), F32),
+            pltpu.VMEM((PAIR, HALF), F32),
             pltpu.VMEM((8, HALF), F32),
             pltpu.VMEM((8, HALF), F32),
             pltpu.VMEM((COLS, RATIO + 2, TOKENS, HEAD), BF16),
@@ -491,7 +490,6 @@
             pltpu.VMEM((COLS, HEAD + SUMROWS, HEAD), BF16),
             pltpu.VMEM((COLS, HEAD + SUMROWS, HEAD), BF16),
             pltpu.VMEM((COLS, HEAD + SUMROWS, HEAD), BF16),
-            pltpu.VMEM((GROUPS, 8, HEAD), jnp.int32),
             pltpu.SMEM((GROUPS, 8, HEAD), jnp.int32),
             dma((COLS, GROUPS)), dma((COLS, GROUPS)), dma((COLS + 3,)),
             dma((GROUPS,)), dma((GROUPS,)), dma((GROUPS,)),

time: 77.5 us -> 73.5 us (0.948)
  Pallas kernels: 74.8 us -> 71.1 us
    pallas_call x1, Pallas kernels: 74.8 us -> 71.1 us  [shards(): pl.pallas_call(kernel, out_shape=jax.ShapeDtypeStruct((TOKENS, COLS * RAT...]
where the time goes in v5:
time: 73.5 us; the launch traced here: 73.4 us
  Pallas kernels  71.1 us (97%)
  other arithmetic  1.62 us (2%)
    pallas_call x1, Pallas kernels, shards(): pl.pallas_call(kernel, out_shape=jax.ShapeDtypeStruct((TOKENS, COLS * RAT...  71.1 us
    broadcast_in_dim x1, other arithmetic, shards(): return result.astype(BF16)[None]  1.62 us

profile of v5, /device:TPU:1, one launch (start us, length us, event | category | flops | bytes accessed | tf_op | source)
XLA Modules:
  0.0 73.4 jit_solution(11280807040868008050)
XLA Ops:
  0.7 71.1 %spanned.1 = f32[16,4096]{1,0:T(8,128)} custom-call(s32[1,48]{1,0:T(1,128)} %bitcast.11, s32[1,48]{1,0:T(1,128)} %slots.1, f32[1,128]{1,0:T(1,128)} %constant.2.clone.freq, bf16[16,4096]{1,0:T(8,128)(2,1)} %bitcast.9, bf16[16,1024]{1,0:T(8,128)(2,1)} %bitcast.10, f32[1,128]{1,0:T(1,128)} %bitcast.12, f32[1,128]{1,0:T(1,128)} %bitcast.13, s32[1]{0:T(128)S(6)} %copy.10.plen, ...), custom_call_target="tpu_custom_call" | custom-call | tf_op jit(solution)/shard_map/spanned/pallas_call | solution.py:462
  71.8 1.6 %convert_bitcast_fusion = bf16[1,16,4096]{2,1,0:T(8,128)(2,1)} fusion(f32[16,4096]{1,0:T(8,128)} %spanned.1), kind=kLoop, calls=%fused_computation | loop fusion | flops 65536 | bytes 393216 | tf_op jit(solution)/shard_map/broadcast_in_dim | solution.py:510

commit v6 on v5

--- a/solution.py
+++ b/solution.py
@@ -88,6 +88,18 @@
     tab[1:2, :] = place
     tab[2:8, :] = jnp.zeros((6, HEAD), jnp.int32)
 
+    pl.semaphore_wait(barrier, len(partners))
+
+    def req_copy(d):
+        to = rot(g + d, GROUPS)
+        return pltpu.make_async_remote_copy(
+            src_ref=tab, dst_ref=reqs.at[g], send_sem=rsend.at[d], recv_sem=rrecv.at[d],
+            device_id=(to, z, x), device_id_type=MESH,
+        )
+
+    for d in range(1, GROUPS):
+        req_copy(d).start()
+
     token_at = limit + (z * COLS + x) * TOKENS + lax.broadcasted_iota(jnp.int32, (TOKENS, HEAD), 0)
     angles = token_at.astype(F32) * freq[...]
     cosf = jnp.cos(angles)
@@ -112,15 +124,6 @@
         qsend[i, RATIO] = part.astype(BF16)
         qsend[i, RATIO + 1] = skv[:, (COLS + i) * HEAD : (COLS + i + 1) * HEAD]
 
-    pl.semaphore_wait(barrier, len(partners))
-
-    def req_copy(d):
-        to = rot(g + d, GROUPS)
-        return pltpu.make_async_remote_copy(
-            src_ref=tab, dst_ref=reqs.at[g], send_sem=rsend.at[d], recv_sem=rrecv.at[d],
-            device_id=(to, z, x), device_id_type=MESH,
-        )
-
     mine = z * COLS + x
 
     def q_copy(k):
@@ -130,8 +133,6 @@
             device_id=(g, z, to), device_id_type=MESH,
         )
 
-    for d in range(1, GROUPS):
-        req_copy(d).start()
     for k in range(1, COLS):
         q_copy(k).start()
 

time: 73.5 us -> 72.6 us (0.988)
  Pallas kernels: 71.1 us -> 70.2 us
    pallas_call x1, Pallas kernels: 71.1 us -> 70.2 us  [shards(): pl.pallas_call(kernel, out_shape=jax.ShapeDtypeStruct((TOKENS, COLS * RAT...]
where the time goes in v6:
time: 72.6 us; the launch traced here: 72.5 us
  Pallas kernels  70.2 us (97%)
  other arithmetic  1.62 us (2%)
    pallas_call x1, Pallas kernels, shards(): pl.pallas_call(kernel, out_shape=jax.ShapeDtypeStruct((TOKENS, COLS * RAT...  70.2 us
    broadcast_in_dim x1, other arithmetic, shards(): return result.astype(BF16)[None]  1.62 us

profile of v6, /device:TPU:1, one launch (start us, length us, event | category | flops | bytes accessed | tf_op | source)
XLA Modules:
  0.0 72.5 jit_solution(14725832515569565552)
XLA Ops:
  0.7 70.2 %spanned.1 = f32[16,4096]{1,0:T(8,128)} custom-call(s32[1,48]{1,0:T(1,128)} %bitcast.11, s32[1,48]{1,0:T(1,128)} %slots.1, f32[1,128]{1,0:T(1,128)} %constant.2.clone.freq, bf16[16,4096]{1,0:T(8,128)(2,1)} %bitcast.9, bf16[16,1024]{1,0:T(8,128)(2,1)} %bitcast.10, f32[1,128]{1,0:T(1,128)} %bitcast.12, f32[1,128]{1,0:T(1,128)} %bitcast.13, s32[1]{0:T(128)S(6)} %copy.10.plen, ...), custom_call_target="tpu_custom_call" | custom-call | tf_op jit(solution)/shard_map/spanned/pallas_call | solution.py:463
  70.9 1.6 %convert_bitcast_fusion = bf16[1,16,4096]{2,1,0:T(8,128)(2,1)} fusion(f32[16,4096]{1,0:T(8,128)} %spanned.1), kind=kLoop, calls=%fused_computation | loop fusion | flops 65536 | bytes 393216 | tf_op jit(solution)/shard_map/broadcast_in_dim | solution.py:511
